TPU v7x, 128 devices: a whole 4x4x4 slice. The times are simulated.
128 devices in a mesh: section: 2 (over x_hi), expert: 16 (over y, z), replica: 4 (over x_lo, core).
Axes of the slice: x: 4 (x_hi: 2, x_lo: 2; x = x_hi * 2 + x_lo), y: 4, z: 4, core: 2. Of those that a mesh axis runs over, the one named last changes fastest.
Arguments:
- boundary: bfloat16 [2, 2, 128, 50, 768], P('section', None, ('expert', 'replica')), may hold values from -6 to 6
- routes: int32 [2, 2, 128, 50, 2], P('section', None, ('expert', 'replica')), may hold values from 0 to 31, all different within a row; in each aligned block of 100 rows (0 to 99, 100 to 199, ..., all dimensions but the last counted through in order) at most 9 rows name the same one
- norm_gains: bfloat16 [2, 2, 768], P('section', None, 'expert'), may hold values from 0.25 to 1.75
- norm_biases: bfloat16 [2, 2, 768], P('section', None, 'expert'), may hold values from -3 to 3
- attend_weight: bfloat16 [2, 768, 2304], P('section', 'expert'), may hold values from -0.21875 to 0.21875
- output_weight: bfloat16 [2, 768, 768], P('section', 'expert'), may hold values from -0.875 to 0.875
- router_weight: bfloat16 [2, 768, 32], P('section', 'expert'), may hold values from -0.21875 to 0.21875
- expert_in: bfloat16 [2, 32, 768, 3072], P('section', 'expert', None, 'replica'), may hold values from -0.21875 to 0.21875
- expert_out: bfloat16 [2, 32, 3072, 768], P('section', 'expert', 'replica'), may hold values from -0.15625 to 0.15625
Outputs:
- results: bfloat16 [2, 2, 128, 50, 768], P('section', None, ('expert', 'replica'))
- gains_grad: float32 [2, 2, 768], P('section', None, 'expert')
- biases_grad: float32 [2, 2, 768], P('section', None, 'expert')
- attend_grad: float32 [2, 768, 2304], P('section', 'expert')
- output_grad: float32 [2, 768, 768], P('section', 'expert')
- router_grad: float32 [2, 768, 32], P('section', 'expert')
- expert_in_grad: float32 [2, 32, 768, 3072], P('section', 'expert', None, 'replica')
- expert_out_grad: float32 [2, 32, 3072, 768], P('section', 'expert', 'replica')
Inputs may be any that keep to these rules, and one draw needn't show every extreme that they name: `routes`: in each layer and micro-batch, the rows of one data index (2 images, both choices) name any one expert at most 9 times, and some expert reaches 9; a token's two experts differ.
All inputs are finite; a program needn't handle non-finite values.
Results may differ from a plain program's by a relative error of at most 0.029.
Values may be sent and summed in bfloat16 or wider, within the bound.
A program may use at most 192 MiB of HBM per device.

v0:
```python
import math

import jax
import jax.numpy as jnp
from jax import lax
from jax.sharding import PartitionSpec as P

D = 768
HEADS = 12
HEAD_DIM = 64
S = 50


EPSILON = 1e-06


def passed_along(value, axis, by):
    length = lax.axis_size(axis)
    pairs = [(i, i + by) for i in range(length) if 0 <= i + by < length]
    return lax.ppermute(value, axis, pairs)


def as_sent(value):
    return jax.tree.map(lambda a: a.astype(jnp.bfloat16) if a.dtype == jnp.float32 else a, value)


def norm_apply(inputs, gain_vec, bias_vec):
    centre = jnp.mean(inputs, axis=-1, keepdims=True)
    spread = jnp.mean(jnp.square(inputs - centre), axis=-1, keepdims=True)
    return (inputs - centre) * lax.rsqrt(spread + EPSILON) * gain_vec + bias_vec


def gelu_tanh(pre_act):
    return jax.nn.gelu(pre_act, approximate=True)


def dispatch_tables(route_ids, total_experts, capacity):
    onehot = (route_ids[:, :, None] == jnp.arange(total_experts, dtype=jnp.int32)).astype(jnp.int32)
    flatten = onehot.reshape(-1, total_experts)
    before = jnp.cumsum(flatten, axis=0) - flatten
    slot_at = jnp.sum(before * flatten, axis=-1).reshape(route_ids.shape)
    target = route_ids * capacity + slot_at
    places = jnp.arange(total_experts * capacity, dtype=jnp.int32)[:, None]
    pick_first = (target[None, :, 0] == places).astype(jnp.bfloat16)
    pick_second = (target[None, :, 1] == places).astype(jnp.bfloat16)
    return (pick_first, pick_second)


def split_heads(joint_proj, images):
    queries = joint_proj[:, :D].reshape(images, S, HEADS, HEAD_DIM)
    keys_in = joint_proj[:, D : 2 * D].reshape(images, S, HEADS, HEAD_DIM)
    values = joint_proj[:, 2 * D :].reshape(images, S, HEADS, HEAD_DIM)
    return (queries, keys_in, values)


def layer_forward(dense_set, expert_pair, tokens, route_ids, capacity):
    gain_rows, bias_rows, attend_w, output_w, router_w = dense_set
    weight_in, weight_out = expert_pair
    row_count = tokens.shape[0]
    images = row_count // S
    scaling = 1.0 / math.sqrt(HEAD_DIM)
    inputs = tokens.astype(jnp.float32)
    normed_one = norm_apply(
        inputs, gain_rows[0].astype(jnp.float32), bias_rows[0].astype(jnp.float32)
    ).astype(jnp.bfloat16)
    joint_proj = jnp.dot(normed_one, attend_w, preferred_element_type=jnp.float32).astype(
        jnp.bfloat16
    )
    queries, keys_in, values = split_heads(joint_proj, images)
    scores = (
        jnp.einsum("nqhc,nkhc->nhqk", queries, keys_in, preferred_element_type=jnp.float32)
        * scaling
    )
    row_max = jnp.max(scores, axis=-1, keepdims=True)
    raised = jnp.exp(scores - row_max)
    row_total = jnp.sum(raised, axis=-1, keepdims=True)
    log_total = row_max + jnp.log(row_total)
    attn_prob = (raised / row_total).astype(jnp.bfloat16)
    mixed_heads = jnp.einsum(
        "nhqk,nkhc->nqhc", attn_prob, values, preferred_element_type=jnp.float32
    )
    mixed_heads = mixed_heads.reshape(row_count, D).astype(jnp.bfloat16)
    hidden = inputs + jnp.dot(mixed_heads, output_w, preferred_element_type=jnp.float32)
    normed_two = norm_apply(
        hidden, gain_rows[1].astype(jnp.float32), bias_rows[1].astype(jnp.float32)
    ).astype(jnp.bfloat16)
    logits = jnp.dot(normed_two, router_w, preferred_element_type=jnp.float32)
    chosen = jnp.take_along_axis(logits, route_ids, axis=1)
    gate_vals = jax.nn.softmax(chosen, axis=-1)
    total_experts = router_w.shape[1]
    pick_first, pick_second = dispatch_tables(route_ids, total_experts, capacity)
    groups = lax.axis_size("expert")
    sending = jnp.dot(
        pick_first + pick_second, normed_two, preferred_element_type=jnp.float32
    ).astype(jnp.bfloat16)
    sending = sending.reshape(groups, total_experts // groups, capacity, D)
    slab_all = lax.all_gather(
        lax.all_to_all(sending, "expert", split_axis=0, concat_axis=0, tiled=True),
        "replica",
        axis=0,
        tiled=True,
    )
    pre_act = jnp.einsum("nesd,edh->nesh", slab_all, weight_in, preferred_element_type=jnp.float32)
    active = gelu_tanh(pre_act).astype(jnp.bfloat16)
    partial_value = jnp.einsum(
        "nesh,ehd->nesd", active, weight_out, preferred_element_type=jnp.float32
    )
    produced = lax.psum_scatter(
        partial_value.astype(jnp.bfloat16), "replica", scatter_dimension=0, tiled=True
    )
    received, pre_act, active, produced = (slab_all, pre_act, active, produced)
    returned = lax.all_to_all(produced, "expert", split_axis=0, concat_axis=0, tiled=True).reshape(
        -1, D
    )
    first_rows = jnp.einsum("pr,pd->rd", pick_first, returned, preferred_element_type=jnp.float32)
    second_rows = jnp.einsum("pr,pd->rd", pick_second, returned, preferred_element_type=jnp.float32)
    output = hidden + (gate_vals[:, 0:1] * first_rows + gate_vals[:, 1:2] * second_rows)
    stored = dict(
        inputs=inputs,
        normed_one=normed_one,
        joint_proj=joint_proj,
        log_total=log_total,
        mixed_heads=mixed_heads,
        hidden=hidden,
        normed_two=normed_two,
        gate_vals=gate_vals,
        first_rows=first_rows.astype(jnp.bfloat16),
        second_rows=second_rows.astype(jnp.bfloat16),
        pick_first=pick_first,
        pick_second=pick_second,
        route_ids=route_ids,
        received=received,
        pre_act=pre_act,
        active=active,
    )
    return (output, stored)


def layer_backward(dense_set, expert_pair, stored, cotangent, in_range):
    gain_rows, bias_rows, attend_w, output_w, router_w = dense_set
    weight_in, weight_out = expert_pair
    row_count = cotangent.shape[0]
    images = row_count // S
    scaling = 1.0 / math.sqrt(HEAD_DIM)
    total_experts = router_w.shape[1]
    gate_vals = stored["gate_vals"]
    pick_first = stored["pick_first"]
    pick_second = stored["pick_second"]
    first_send = (gate_vals[:, 0:1] * cotangent).astype(jnp.bfloat16)
    second_send = (gate_vals[:, 1:2] * cotangent).astype(jnp.bfloat16)
    gate_grad = jnp.stack(
        [
            jnp.sum(cotangent * stored["first_rows"].astype(jnp.float32), axis=-1),
            jnp.sum(cotangent * stored["second_rows"].astype(jnp.float32), axis=-1),
        ],
        axis=1,
    )
    chosen_grad = gate_vals * (gate_grad - jnp.sum(gate_vals * gate_grad, axis=-1, keepdims=True))
    onehot = (stored["route_ids"][:, :, None] == jnp.arange(total_experts, dtype=jnp.int32)).astype(
        jnp.float32
    )
    logit_grad = jnp.sum(chosen_grad[:, :, None] * onehot, axis=1).astype(jnp.bfloat16)
    router_g = jnp.dot(stored["normed_two"].T, logit_grad, preferred_element_type=jnp.float32)
    router_part = jnp.dot(logit_grad, router_w.T, preferred_element_type=jnp.float32)
    received = stored["received"]
    groups = lax.axis_size("expert")
    grad_send = jnp.einsum(
        "pr,rd->pd", pick_first, first_send, preferred_element_type=jnp.float32
    ) + jnp.einsum("pr,rd->pd", pick_second, second_send, preferred_element_type=jnp.float32)
    grad_send = grad_send.astype(jnp.bfloat16).reshape(groups, total_experts // groups, -1, D)
    grad_recv = lax.all_to_all(grad_send, "expert", split_axis=0, concat_axis=0, tiled=True)
    grad_all = lax.all_gather(grad_recv, "replica", axis=0, tiled=True)
    act_grad = jnp.einsum(
        "nesd,ehd->nesh", grad_all, weight_out, preferred_element_type=jnp.float32
    )
    pre_grad = jax.vjp(gelu_tanh, stored["pre_act"])[1](act_grad)[0].astype(jnp.bfloat16)
    back_part = jnp.einsum(
        "nesh,edh->nesd", pre_grad, weight_in, preferred_element_type=jnp.float32
    )
    back = lax.psum_scatter(
        back_part.astype(jnp.bfloat16), "replica", scatter_dimension=0, tiled=True
    )
    back_home = lax.all_to_all(back, "expert", split_axis=0, concat_axis=0, tiled=True).reshape(
        -1, D
    )
    first_back = jnp.einsum("pr,pd->rd", pick_first, back_home, preferred_element_type=jnp.float32)
    second_back = jnp.einsum(
        "pr,pd->rd", pick_second, back_home, preferred_element_type=jnp.float32
    )
    normed_grad = router_part + (first_back + second_back)
    pull_two = jax.vjp(
        norm_apply,
        stored["hidden"],
        gain_rows[1].astype(jnp.float32),
        bias_rows[1].astype(jnp.float32),
    )[1]
    hidden_part, gain_two, bias_two = pull_two(normed_grad)
    hidden_grad = cotangent + hidden_part
    hidden_b = hidden_grad.astype(jnp.bfloat16)
    output_g = jnp.dot(stored["mixed_heads"].T, hidden_b, preferred_element_type=jnp.float32)
    mixed_grad = jnp.dot(hidden_b, output_w.T, preferred_element_type=jnp.float32).astype(
        jnp.bfloat16
    )
    mixed_grad = mixed_grad.reshape(images, S, HEADS, HEAD_DIM)
    queries, keys_in, values = split_heads(stored["joint_proj"], images)
    scores = (
        jnp.einsum("nqhc,nkhc->nhqk", queries, keys_in, preferred_element_type=jnp.float32)
        * scaling
    )
    attn_prob = jnp.exp(scores - stored["log_total"])
    prob_b = attn_prob.astype(jnp.bfloat16)
    value_grad = jnp.einsum(
        "nhqk,nqhc->nkhc", prob_b, mixed_grad, preferred_element_type=jnp.float32
    )
    prob_grad = jnp.einsum(
        "nqhc,nkhc->nhqk", mixed_grad, values, preferred_element_type=jnp.float32
    )
    row_delta = jnp.sum(attn_prob * prob_grad, axis=-1, keepdims=True)
    score_grad = (attn_prob * (prob_grad - row_delta) * scaling).astype(jnp.bfloat16)
    query_grad = jnp.einsum(
        "nhqk,nkhc->nqhc", score_grad, keys_in, preferred_element_type=jnp.float32
    )
    key_grad = jnp.einsum(
        "nhqk,nqhc->nkhc", score_grad, queries, preferred_element_type=jnp.float32
    )
    joint_grad = jnp.concatenate(
        [
            query_grad.reshape(row_count, D),
            key_grad.reshape(row_count, D),
            value_grad.reshape(row_count, D),
        ],
        axis=1,
    ).astype(jnp.bfloat16)
    attend_g = jnp.dot(stored["normed_one"].T, joint_grad, preferred_element_type=jnp.float32)
    normed_one_grad = jnp.dot(joint_grad, attend_w.T, preferred_element_type=jnp.float32)
    pull_one = jax.vjp(
        norm_apply,
        stored["inputs"],
        gain_rows[0].astype(jnp.float32),
        bias_rows[0].astype(jnp.float32),
    )[1]
    input_part, gain_one, bias_one = pull_one(normed_one_grad)
    input_grad = hidden_grad + input_part
    grad_set = (
        jnp.stack([gain_one, gain_two]),
        jnp.stack([bias_one, bias_two]),
        attend_g,
        output_g,
        router_g,
    )
    dense_grads = tuple((grad_item * in_range for grad_item in grad_set))
    mask_bf = in_range.astype(jnp.bfloat16)
    expert_piece = (received, pre_grad * mask_bf, stored["active"], grad_all * mask_bf)
    return (input_grad, dense_grads, expert_piece)


def add_trees(running, addend):
    if running is None:
        return addend
    return jax.tree.map(lambda summand, extra: summand + extra, running, addend)


def shards(
    boundary,
    routes,
    norm_gains,
    norm_biases,
    attend_weight,
    output_weight,
    router_weight,
    expert_in,
    expert_out,
):
    section_at = lax.axis_index("section")
    micro_count = boundary.shape[1]
    row_count = boundary.shape[2] * boundary.shape[3]
    local_in = boundary[0].reshape(micro_count, row_count, D)
    local_routes = routes[0].reshape(micro_count, row_count, 2)
    total_experts = router_weight.shape[2]
    capacity = max(2, 3 * row_count // total_experts)
    expert_pair = (expert_in[0], expert_out[0])

    def gather_dense():
        return (
            lax.all_gather(norm_gains[0], "expert", axis=1, tiled=True),
            lax.all_gather(norm_biases[0], "expert", axis=1, tiled=True),
            lax.all_gather(attend_weight[0], "expert", axis=0, tiled=True),
            lax.all_gather(output_weight[0], "expert", axis=0, tiled=True),
            lax.all_gather(router_weight[0], "expert", axis=0, tiled=True),
        )

    saved_list = []
    outputs = []
    incoming = jnp.zeros((row_count, D), jnp.bfloat16)
    for tick_no in range(micro_count + 1):
        dense_set = gather_dense()
        micro_at = jnp.clip(tick_no - section_at, 0, micro_count - 1)
        own_input = lax.dynamic_index_in_dim(local_in, micro_at, 0, keepdims=False)
        tokens_now = jnp.where(section_at == 0, own_input, incoming)
        route_now = lax.dynamic_index_in_dim(local_routes, micro_at, 0, keepdims=False)
        produced, stored = layer_forward(dense_set, expert_pair, tokens_now, route_now, capacity)
        sent_out = produced.astype(jnp.bfloat16)
        outputs.append(sent_out)
        saved_list.append(stored)
        if tick_no < micro_count:
            incoming = passed_along(sent_out, "section", 1)
    saved_all = jax.tree.map(lambda *leaves: jnp.stack(leaves), *saved_list)
    shard_sum = None
    grads_out = []
    expert_parts = []
    back_in = jnp.zeros((row_count, D), jnp.bfloat16)
    for tick_no in range(micro_count + 1):
        dense_set = gather_dense()
        micro_at = tick_no - 1 + section_at
        in_range = ((micro_at >= 0) & (micro_at <= micro_count - 1)).astype(jnp.float32)
        saved_at = jnp.clip(micro_at + section_at, 0, micro_count)
        stored = jax.tree.map(
            lambda stacked: lax.dynamic_index_in_dim(stacked, saved_at, 0, keepdims=False),
            saved_all,
        )
        own_cot = lax.dynamic_index_in_dim(
            local_in, jnp.clip(micro_at, 0, micro_count - 1), 0, keepdims=False
        )
        cotangent = jnp.where(section_at == 1, own_cot, back_in).astype(jnp.float32)
        input_grad, dense_grads, expert_piece = layer_backward(
            dense_set, expert_pair, stored, cotangent, in_range
        )
        rounded = input_grad.astype(jnp.bfloat16)
        grads_out.append(rounded)
        expert_parts.append(expert_piece)
        shard_sum = add_trees(
            shard_sum,
            (
                lax.psum_scatter(
                    dense_grads[0].astype(jnp.bfloat16), "expert", scatter_dimension=1, tiled=True
                ).astype(jnp.float32),
                lax.psum_scatter(
                    dense_grads[1].astype(jnp.bfloat16), "expert", scatter_dimension=1, tiled=True
                ).astype(jnp.float32),
                lax.psum_scatter(
                    dense_grads[2].astype(jnp.bfloat16), "expert", scatter_dimension=0, tiled=True
                ).astype(jnp.float32),
                lax.psum_scatter(
                    dense_grads[3].astype(jnp.bfloat16), "expert", scatter_dimension=0, tiled=True
                ).astype(jnp.float32),
                lax.psum_scatter(
                    dense_grads[4].astype(jnp.bfloat16), "expert", scatter_dimension=0, tiled=True
                ).astype(jnp.float32),
            ),
        )
        if tick_no < micro_count:
            back_in = passed_along(rounded, "section", -1)
    summed = jax.tree.map(
        lambda part: part.astype(jnp.float32), lax.psum(as_sent(shard_sum), "replica")
    )
    received_all = jnp.stack([piece_set[0] for piece_set in expert_parts])
    pre_grad_all = jnp.stack([piece_set[1] for piece_set in expert_parts])
    active_all = jnp.stack([piece_set[2] for piece_set in expert_parts])
    recv_all = jnp.stack([piece_set[3] for piece_set in expert_parts])
    first_grad = jnp.einsum(
        "tnesd,tnesh->edh", received_all, pre_grad_all, preferred_element_type=jnp.float32
    )
    second_grad = jnp.einsum(
        "tnesh,tnesd->ehd", active_all, recv_all, preferred_element_type=jnp.float32
    )
    owned_in, owned_out = (first_grad, second_grad)
    final_pass = jnp.stack(outputs[1:])
    final_grads = jnp.stack(grads_out[1:])
    merged = jnp.where(section_at == 0, final_grads, final_pass).reshape(boundary.shape)
    return (
        merged,
        summed[0][None],
        summed[1][None],
        summed[2][None],
        summed[3][None],
        summed[4][None],
        owned_in[None],
        owned_out[None],
    )


def solution(mesh):
    in_specs = (
        P("section", None, ("expert", "replica"), None, None),
        P("section", None, ("expert", "replica"), None, None),
        P("section", None, "expert"),
        P("section", None, "expert"),
        P("section", "expert", None),
        P("section", "expert", None),
        P("section", "expert", None),
        P("section", "expert", None, "replica"),
        P("section", "expert", "replica", None),
    )
    out_specs = (
        P("section", None, ("expert", "replica"), None, None),
        P("section", None, "expert"),
        P("section", None, "expert"),
        P("section", "expert", None),
        P("section", "expert", None),
        P("section", "expert", None),
        P("section", "expert", None, "replica"),
        P("section", "expert", "replica", None),
    )
    return jax.shard_map(shards, mesh=mesh, in_specs=in_specs, out_specs=out_specs, check_vma=False)
```

profile of v0, /device:TPU:1, one launch (start us, length us, event | category | flops | bytes accessed | tf_op | source)
XLA Modules:
  0.0 1490.3 jit_solution(17595352233752120731)
XLA Ops:
  10.7 21.8 %all-gather.1 = bf16[1,2,768]{1,0,2:T(2,128)(2,1)S(1)} all-gather(bf16[1,2,48]{1,0,2:T(2,128)(2,1)S(1)} %copy.534), channel_id=3, replica_groups=mesh['section'=2,'expert'=16,'replica'=4] {'expert'}, dimensions={2}, use_global_device_ids=true | all-gather | bytes 3264 | tf_op jit(solution)/shard_map/all_gather | solution.py:286
  32.5 4.6 fusion.215
  37.9 21.1 %all-gather = bf16[1,2,768]{1,0,2:T(2,128)(2,1)S(1)} all-gather(bf16[1,2,48]{1,0,2:T(2,128)(2,1)S(1)} %copy.533), channel_id=2, replica_groups=mesh['section'=2,'expert'=16,'replica'=4] {'expert'}, dimensions={2}, use_global_device_ids=true | all-gather | bytes 3264 | tf_op jit(solution)/shard_map/all_gather | solution.py:285
  65.1 4.6 fusion.216
  81.4 25.4 %all-gather.28.cloned.1.call-done = bf16[1,768,768]{2,1,0:T(8,128)(2,1)} async-done(((bf16[1,48,768]{2,1,0:T(8,128)(2,1)}), bf16[1,768,768]{2,1,0:T(8,128)(2,1)}) %all-gather.28.cloned.1.call-update) | async-done | bytes 1179664 | tf_op jit(solution)/shard_map/all_gather | solution.py:288
  112.1 13.0 all_to_all.60
  126.4 27.2 %all-gather.14.cloned.1.call-done = bf16[64,2,9,768]{3,0,2,1:T(8,128)(2,1)} async-done(((bf16[16,2,9,768]{3,0,2,1:T(8,128)(2,1)}), bf16[64,2,9,768]{3,0,2,1:T(8,128)(2,1)}) %all-gather.14.cloned.1.call-update) | async-done | bytes 1769488 | tf_op jit(solution)/shard_map/all_gather | solution.py:97
  153.7 3.7 fusion.110
  162.3 19.0 %all-gather.4 = bf16[1,768,32]{2,0,1:T(2,128)(2,1)S(1)} all-gather(bf16[1,48,32]{2,0,1:T(2,128)(2,1)S(1)} %copy.540), channel_id=6, replica_groups=mesh['section'=2,'expert'=16,'replica'=4] {'expert'}, dimensions={1}, use_global_device_ids=true | all-gather | bytes 52224 | tf_op jit(solution)/shard_map/all_gather | solution.py:289
  190.8 6.5 all-to-all-start.1
  197.4 8.2 all-to-all-done.1
  209.2 4.3 collective-permute-start
  236.9 11.4 all_to_all.61
  249.4 32.0 %all-gather.16.cloned.1.call-done = bf16[64,2,9,768]{3,0,2,1:T(8,128)(2,1)} async-done(((bf16[16,2,9,768]{3,0,2,1:T(8,128)(2,1)}), bf16[64,2,9,768]{3,0,2,1:T(8,128)(2,1)}) %all-gather.16.cloned.1.call-update) | async-done | bytes 1769488 | tf_op jit(solution)/shard_map/all_gather | solution.py:97
  281.4 3.7 fusion.108
  293.2 3.6 gather_fusion.1
  300.9 15.4 %reduce-scatter.24.cloned.1.call-done = bf16[16,2,9,768]{3,0,2,1:T(8,128)(2,1)} async-done(((bf16[64,2,9,768]{3,0,2,1:T(8,128)(2,1)}), bf16[16,2,9,768]{3,0,2,1:T(8,128)(2,1)}) %reduce-scatter.24.cloned.1.call-update) | async-done | bytes 442384 | tf_op jit(solution)/shard_map/reduce_scatter | solution.py:108
  318.4 6.9 all-to-all-start.3
  326.6 8.5 all-to-all-done.3
  342.7 4.3 collective-permute-start.1
  373.0 11.6 all_to_all.62
  385.7 28.8 %all-gather.18.cloned.1.call-done = bf16[64,2,9,768]{3,0,2,1:T(8,128)(2,1)} async-done(((bf16[16,2,9,768]{3,0,2,1:T(8,128)(2,1)}), bf16[64,2,9,768]{3,0,2,1:T(8,128)(2,1)}) %all-gather.18.cloned.1.call-update) | async-done | bytes 1769488 | tf_op jit(solution)/shard_map/all_gather | solution.py:97
  414.5 3.7 fusion.106
  433.5 3.6 gather_fusion.2
  441.3 8.1 reduce-scatter.26.cloned.1.call-done
  451.5 6.7 all-to-all-start.5
  459.0 9.1 all-to-all-done.5
  485.8 11.5 all_to_all.63
  500.8 9.3 pad_maximum_fusion
  510.1 15.1 %all-gather.20.cloned.1.call-done = bf16[64,2,9,768]{3,0,2,1:T(8,128)(2,1)} async-done(((bf16[16,2,9,768]{3,0,2,1:T(8,128)(2,1)}), bf16[64,2,9,768]{3,0,2,1:T(8,128)(2,1)}) %all-gather.20.cloned.1.call-update) | async-done | bytes 1769488 | tf_op jit(solution)/shard_map/all_gather | solution.py:172
  525.2 5.8 fusion.31
  552.6 8.8 reduce-scatter.28.cloned.1.call-done
  563.6 6.7 all-to-all-start.7
  574.6 5.6 all-to-all-done.7
  621.8 4.3 multiply_reduce_fusion.8
  630.7 6.2 collective-permute-done.2
  645.9 11.6 all_to_all.64
  658.4 25.8 %all-gather.22.cloned.1.call-done = bf16[64,2,9,768]{3,0,2,1:T(8,128)(2,1)} async-done(((bf16[16,2,9,768]{3,0,2,1:T(8,128)(2,1)}), bf16[64,2,9,768]{3,0,2,1:T(8,128)(2,1)}) %all-gather.22.cloned.1.call-update) | async-done | bytes 1769488 | tf_op jit(solution)/shard_map/all_gather | solution.py:172
  684.2 5.8 fusion.38
  709.0 11.5 reduce-scatter.30.cloned.1.call-done
  722.5 6.7 all-to-all-start.9
  733.2 5.8 all-to-all-done.9
  780.8 4.2 multiply_reduce_fusion.6
  788.7 6.2 collective-permute-done.3
  803.9 11.6 all_to_all.65
  816.4 25.9 %all-gather.24.cloned.1.call-done = bf16[64,2,9,768]{3,0,2,1:T(8,128)(2,1)} async-done(((bf16[16,2,9,768]{3,0,2,1:T(8,128)(2,1)}), bf16[64,2,9,768]{3,0,2,1:T(8,128)(2,1)}) %all-gather.24.cloned.1.call-update) | async-done | bytes 1769488 | tf_op jit(solution)/shard_map/all_gather | solution.py:172
  842.2 5.8 fusion.45
  869.3 9.1 reduce-scatter.32.cloned.1.call-done
  880.5 6.9 all-to-all-start.11
  891.2 6.0 all-to-all-done.11
  914.1 3.9 multiply_convert_fusion.2
  918.1 4.1 multiply_convert_fusion.1
  926.1 4.4 fusion.495
  987.5 4.0 multiply_convert_fusion
  1005.6 8.0 fusion.117
  1013.7 8.0 fusion.112
  1028.5 3.5 reduce-scatter.42.cloned.1.call-done
  1032.0 76.7 %reduce-scatter.44.cloned.1.call-done = bf16[48,768]{1,0:T(8,128)(2,1)} async-done(((bf16[768,768]{1,0:T(8,128)(2,1)}), bf16[48,768]{1,0:T(8,128)(2,1)}) %reduce-scatter.44.cloned.1.call-update) | async-done | bytes 73744 | tf_op jit(solution)/shard_map/reduce_scatter | solution.py:343
  1110.3 78.2 %reduce-scatter.34.cloned.1.call-done = bf16[48,2304]{1,0:T(8,128)(2,1)} async-done(((bf16[768,2304]{1,0:T(8,128)(2,1)}), bf16[48,2304]{1,0:T(8,128)(2,1)}) %reduce-scatter.34.cloned.1.call-update) | async-done | bytes 221200 | tf_op jit(solution)/shard_map/reduce_scatter | solution.py:340
  1188.5 79.9 %reduce-scatter.36.cloned.1.call-done = bf16[48,2304]{1,0:T(8,128)(2,1)} async-done(((bf16[768,2304]{1,0:T(8,128)(2,1)}), bf16[48,2304]{1,0:T(8,128)(2,1)}) %reduce-scatter.36.cloned.1.call-update) | async-done | bytes 221200 | tf_op jit(solution)/shard_map/reduce_scatter | solution.py:340
  1268.4 79.7 %reduce-scatter.38.cloned.1.call-done = bf16[48,2304]{1,0:T(8,128)(2,1)} async-done(((bf16[768,2304]{1,0:T(8,128)(2,1)}), bf16[48,2304]{1,0:T(8,128)(2,1)}) %reduce-scatter.38.cloned.1.call-update) | async-done | bytes 221200 | tf_op jit(solution)/shard_map/reduce_scatter | solution.py:340
  1350.0 88.8 %all-reduce.18.cloned.1.call-done = (bf16[2,768]{1,0:T(2,128)(2,1)}, bf16[2,768]{1,0:T(2,128)(2,1)}, bf16[2,768]{1,0:T(2,128)(2,1)}, bf16[2,768]{1,0:T(2,128)(2,...) async-done(((bf16[2,768]{1,0:T(2,128)(2,1)}, ...) | async-done | bytes 165904
  1441.1 7.6 all-reduce.13
  1450.4 29.3 %all-reduce.20.cloned.1.call-done = (bf16[1,48,2304]{2,1,0:T(8,128)(2,1)}, bf16[1,48,768]{2,1,0:T(8,128)(2,1)}) async-done(((bf16[1,48,2304]{2,1,0:T(8,128)(2,1)}, bf16[1,48,768]{2,1,0:T(8,128)(2,1)}), (bf16[1,48,2304]{2,1,0:T(8,128)(2,1)}, bf16[1,48,768]{2,1,0:T(8,128)(2,1)})) %all-reduce.20.cloned.1.call-update) | async-done | bytes 294928 | tf_op jit(solution)/shard_map/psum | solution.py:354
  (798 shorter events, 463.1 us)
Async XLA Ops:
  7.2 152.0 %copy-start = (bf16[1,2,768,768]{3,2,1,0:T(8,128)(2,1)S(1)}, bf16[1,2,768,768]{3,2,1,0:T(8,128)(2,1)}, u32[]{:S(2)}) copy-start(bf16[1,2,768,768]{3,2,1,0:T(8,128)(2,1)} %param.19) | copy-start | bytes 7077892
  7.2 63.2 %all-gather.26.cloned.1.call-start = ((), (), s32[]{:S(2)}) async-start(), calls=%async_computation.42 | async-start | bytes 3760128 | tf_op jit(solution)/shard_map/all_gather | solution.py:287
  7.9 54.8 %copy-start.154 = (s32[1,2,2,50,2]{3,4,2,1,0:T(2,128)S(1)}, s32[1,2,2,50,2]{3,4,2,1,0:T(2,128)}, u32[]{:S(2)}) copy-start(s32[1,2,2,50,2]{3,4,2,1,0:T(2,128)} %param.12) | copy-start | bytes 4804
  7.9 98.9 %all-gather.28.cloned.1.call-start = ((), (), s32[]{:S(2)}) async-start(), calls=%async_computation.43 | async-start | bytes 1253376 | tf_op jit(solution)/shard_map/all_gather | solution.py:288
  8.7 145.0 %all-gather.14.cloned.1.call-start = ((), (), s32[]{:S(2)}) async-start(), calls=%async_computation.24 | async-start | bytes 2211840 | tf_op jit(solution)/shard_map/all_gather | solution.py:97
  37.2 180.6 %copy-start.82 = (f32[768]{0:T(1024)}, f32[768]{0:T(1024)S(1)}, u32[]{:S(2)}) copy-start(f32[768]{0:T(1024)S(1)} %get-tuple-element.82) | copy-start | bytes 9220
  37.2 193.8 %copy-start.79 = (f32[768]{0:T(1024)}, f32[768]{0:T(1024)S(1)}, u32[]{:S(2)}) copy-start(f32[768]{0:T(1024)S(1)} %get-tuple-element.81) | copy-start | bytes 9220
  62.6 44.2 %copy-start.21 = (bf16[1,100,768]{2,1,0:T(8,128)(2,1)}, bf16[1,100,768]{2,1,0:T(8,128)(2,1)S(1)}, u32[]{:S(2)}) copy-start(bf16[1,100,768]{2,1,0:T(8,128)(2,1)S(1)} %get-tuple-element.122) | copy-start | bytes 460804
  63.4 121.3 %copy-start.103 = (s32[1,100,2]{1,2,0:T(2,128)}, s32[1,100,2]{1,2,0:T(2,128)S(1)}, u32[]{:S(2)}) copy-start(s32[1,100,2]{1,2,0:T(2,128)S(1)} %get-tuple-element.133) | copy-start | bytes 2404
  63.4 121.3 %copy-start.104 = (s32[1,100,2]{1,2,0:T(2,128)}, s32[1,100,2]{1,2,0:T(2,128)S(1)}, u32[]{:S(2)}) copy-start(s32[1,100,2]{1,2,0:T(2,128)S(1)} %get-tuple-element.194) | copy-start | bytes 2404
  63.4 125.1 %copy-start.102 = (s32[1,100,2]{1,2,0:T(2,128)}, s32[1,100,2]{1,2,0:T(2,128)S(1)}, u32[]{:S(2)}) copy-start(s32[1,100,2]{1,2,0:T(2,128)S(1)} %get-tuple-element.196) | copy-start | bytes 2404
  69.7 148.1 %copy-start.76 = (f32[768]{0:T(1024)}, f32[768]{0:T(1024)S(1)}, u32[]{:S(2)}) copy-start(f32[768]{0:T(1024)S(1)} %get-tuple-element.80) | copy-start | bytes 9220
  69.7 161.3 %copy-start.69 = (f32[768]{0:T(1024)}, f32[768]{0:T(1024)S(1)}, u32[]{:S(2)}) copy-start(f32[768]{0:T(1024)S(1)} %get-tuple-element.79) | copy-start | bytes 9220
  77.7 31.0 %copy-start.87 = (f32[2,12,50]{2,1,0:T(8,128)}, f32[2,12,50]{2,1,0:T(8,128)S(1)}, u32[]{:S(2)}) copy-start(f32[2,12,50]{2,1,0:T(8,128)S(1)} %get-tuple-element.215) | copy-start | bytes 14404
  77.9 31.0 %copy-start.98 = (f32[2,12,50]{2,1,0:T(8,128)}, f32[2,12,50]{2,1,0:T(8,128)S(1)}, u32[]{:S(2)}) copy-start(f32[2,12,50]{2,1,0:T(8,128)S(1)} %fusion.209) | copy-start | bytes 14404
  77.9 31.7 %copy-start.123 = (s32[100]{0:T(128)S(1)}, s32[100]{0:T(128)}, u32[]{:S(2)}) copy-start(s32[100]{0:T(128)} %get-tuple-element.213) | copy-start | bytes 1204
  77.9 31.7 %copy-start.133 = (s32[100]{0:T(128)S(1)}, s32[100]{0:T(128)}, u32[]{:S(2)}) copy-start(s32[100]{0:T(128)} %get-tuple-element.214) | copy-start | bytes 1204
  108.5 99.7 %copy-start.15 = (f32[100,768]{1,0:T(8,128)}, f32[100,768]{1,0:T(8,128)S(1)}, u32[]{:S(2)}) copy-start(f32[100,768]{1,0:T(8,128)S(1)} %get-tuple-element.218) | copy-start | bytes 921604
  108.5 45.1 %copy-start.147 = (f32[100]{0:T(128)}, f32[100]{0:T(128)S(1)}, u32[]{:S(2)}) copy-start(f32[100]{0:T(128)S(1)} %broadcast_multiply_fusion.10) | copy-start | bytes 1204
  108.7 48.7 %copy-start.158 = (f32[100]{0:T(128)}, f32[100]{0:T(128)S(1)}, u32[]{:S(2)}) copy-start(f32[100]{0:T(128)S(1)} %add_rsqrt_fusion.4) | copy-start | bytes 1204
  126.0 62.7 %reduce-scatter.22.cloned.1.call-start = ((), (), s32[]{:S(2)}) async-start(), calls=%async_computation.25 | async-start | bytes 2211840 | tf_op jit(solution)/shard_map/reduce_scatter | solution.py:108
  159.2 22.4 %copy-start.156 = (s32[100,2,1]{0,1,2:T(2,128)S(1)}, s32[100,2,1]{0,1,2:T(2,128)}, u32[]{:S(2)}) copy-start(s32[100,2,1]{0,1,2:T(2,128)} %get-tuple-element.195) | copy-start | bytes 2404
  162.1 23.2 %copy-start.61 = (bf16[100,768]{1,0:T(8,128)(2,1)S(1)}, bf16[100,768]{1,0:T(8,128)(2,1)}, u32[]{:S(2)}) copy-start(bf16[100,768]{1,0:T(8,128)(2,1)} %copy-done.60) | copy-start | bytes 460804
  188.6 27.1 %copy-start.111 = (f32[100,2]{0,1:T(2,128)}, f32[100,2]{0,1:T(2,128)S(1)}, u32[]{:S(2)}) copy-start(f32[100,2]{0,1:T(2,128)S(1)} %get-tuple-element.139) | copy-start | bytes 2404
  188.6 28.8 %copy-start.130 = (f32[100]{0:T(128)}, f32[100]{0:T(128)S(1)}, u32[]{:S(2)}) copy-start(f32[100]{0:T(128)S(1)} %get-tuple-element.138) | copy-start | bytes 1204
  188.7 28.8 %copy-start.145 = (f32[100]{0:T(128)}, f32[100]{0:T(128)S(1)}, u32[]{:S(2)}) copy-start(f32[100]{0:T(128)S(1)} %fusion.466) | copy-start | bytes 1204
  190.8 14.8 all-to-all-start.1
  197.3 84.0 %all-gather.16.cloned.1.call-start = ((), (), s32[]{:S(2)}) async-start(), calls=%async_computation.26 | async-start | bytes 2211840 | tf_op jit(solution)/shard_map/all_gather | solution.py:97
  209.2 6.5 collective-permute-start
  249.1 67.1 %reduce-scatter.24.cloned.1.call-start = ((), (), s32[]{:S(2)}) async-start(), calls=%async_computation.27 | async-start | bytes 2211840 | tf_op jit(solution)/shard_map/reduce_scatter | solution.py:108
  296.8 43.8 %copy-start.126 = (s32[100]{0:T(128)S(1)}, s32[100]{0:T(128)}, u32[]{:S(2)}) copy-start(s32[100]{0:T(128)} %copy-done.125) | copy-start | bytes 1204
  318.4 32.9 %copy-start.77 = (f32[768]{0:T(1024)S(1)}, f32[768]{0:T(1024)}, u32[]{:S(2)}) copy-start(f32[768]{0:T(1024)} %copy-done.76) | copy-start | bytes 9220
  318.4 32.9 %copy-start.83 = (f32[768]{0:T(1024)S(1)}, f32[768]{0:T(1024)}, u32[]{:S(2)}) copy-start(f32[768]{0:T(1024)} %copy-done.82) | copy-start | bytes 9220
  318.4 16.7 %all-to-all-start.3 = ((bf16[16,2,9,768]{3,1,2,0:T(2,128)(2,1)}), bf16[16,2,9,768]{3,1,2,0:T(2,128)(2,1)}, u32[]{:S(2)}, u32[]{:S(2)}) async-start(bf16[16,2,9,768]{3,1,2,0:T(2,128)(2,1)} %copy.565), calls=%async_computation.5 | async-start | bytes 884736 | tf_op jit(solution)/shard_map/all_to_all | solution.py:112
  325.3 89.2 %all-gather.18.cloned.1.call-start = ((), (), s32[]{:S(2)}) async-start(), calls=%async_computation.28 | async-start | bytes 2211840 | tf_op jit(solution)/shard_map/all_gather | solution.py:97
  342.7 6.5 collective-permute-start.1
  385.4 63.9 %reduce-scatter.26.cloned.1.call-start = ((), (), s32[]{:S(2)}) async-start(), calls=%async_computation.29 | async-start | bytes 2211840 | tf_op jit(solution)/shard_map/reduce_scatter | solution.py:108
  437.1 36.4 %copy-start.127 = (s32[100]{0:T(128)S(1)}, s32[100]{0:T(128)}, u32[]{:S(2)}) copy-start(s32[100]{0:T(128)} %get-tuple-element.205) | copy-start | bytes 1204
  441.3 36.8 %copy-start.117 = (f32[3,100,2]{1,2,0:T(2,128)}, f32[3,100,2]{1,2,0:T(2,128)S(1)}, u32[]{:S(2)}) copy-start(f32[3,100,2]{1,2,0:T(2,128)S(1)} %pad_maximum_fusion.11) | copy-start | bytes 7204
  451.5 16.5 %all-to-all-start.5 = ((bf16[16,2,9,768]{3,1,2,0:T(2,128)(2,1)}), bf16[16,2,9,768]{3,1,2,0:T(2,128)(2,1)}, u32[]{:S(2)}, u32[]{:S(2)}) async-start(bf16[16,2,9,768]{3,1,2,0:T(2,128)(2,1)} %copy.580), calls=%async_computation.8 | async-start | bytes 884736 | tf_op jit(solution)/shard_map/all_to_all | solution.py:112
  458.2 67.0 %all-gather.20.cloned.1.call-start = ((), (), s32[]{:S(2)}) async-start(), calls=%async_computation.30 | async-start | bytes 2211840 | tf_op jit(solution)/shard_map/all_gather | solution.py:172
  479.2 20.2 %copy-start.88 = (f32[2,12,50]{2,1,0:T(8,128)S(1)}, f32[2,12,50]{2,1,0:T(8,128)}, u32[]{:S(2)}) copy-start(f32[2,12,50]{2,1,0:T(8,128)} %copy-done.87) | copy-start | bytes 14404
  498.1 63.3 %reduce-scatter.28.cloned.1.call-start = ((), (), s32[]{:S(2)}) async-start(), calls=%async_computation.31 | async-start | bytes 2211840 | tf_op jit(solution)/shard_map/reduce_scatter | solution.py:180
  549.5 36.0 %copy-start.71 = (f32[768]{0:T(1024)S(1)}, f32[768]{0:T(1024)}, u32[]{:S(2)}) copy-start(f32[768]{0:T(1024)} %copy-done.69) | copy-start | bytes 9220
  550.3 37.6 %copy-start.129 = (f32[100]{0:T(128)}, f32[100]{0:T(128)S(1)}, u32[]{:S(2)}) copy-start(f32[100]{0:T(128)S(1)} %broadcast_multiply_fusion.3) | copy-start | bytes 1204
  563.6 16.6 %all-to-all-start.7 = ((bf16[16,2,9,768]{3,1,2,0:T(2,128)(2,1)}), bf16[16,2,9,768]{3,1,2,0:T(2,128)(2,1)}, u32[]{:S(2)}, u32[]{:S(2)}) async-start(bf16[16,2,9,768]{3,1,2,0:T(2,128)(2,1)} %copy.584), calls=%async_computation.11 | async-start | bytes 884736 | tf_op jit(solution)/shard_map/all_to_all | solution.py:183
  570.3 113.9 %all-gather.22.cloned.1.call-start = ((), (), s32[]{:S(2)}) async-start(), calls=%async_computation.32 | async-start | bytes 2211840 | tf_op jit(solution)/shard_map/all_gather | solution.py:172
  600.4 21.5 %copy-start.78 = (f32[768]{0:T(1024)S(1)}, f32[768]{0:T(1024)}, u32[]{:S(2)}) copy-start(f32[768]{0:T(1024)} %copy-done.76) | copy-start | bytes 9220
  629.4 7.5 collective-permute-start.2
  658.3 62.1 %reduce-scatter.30.cloned.1.call-start = ((), (), s32[]{:S(2)}) async-start(), calls=%async_computation.33 | async-start | bytes 2211840 | tf_op jit(solution)/shard_map/reduce_scatter | solution.py:180
  722.5 16.5 %all-to-all-start.9 = ((bf16[16,2,9,768]{3,1,2,0:T(2,128)(2,1)}), bf16[16,2,9,768]{3,1,2,0:T(2,128)(2,1)}, u32[]{:S(2)}, u32[]{:S(2)}) async-start(bf16[16,2,9,768]{3,1,2,0:T(2,128)(2,1)} %copy.599), calls=%async_computation.14 | async-start | bytes 884736 | tf_op jit(solution)/shard_map/all_to_all | solution.py:183
  729.3 112.9 %all-gather.24.cloned.1.call-start = ((), (), s32[]{:S(2)}) async-start(), calls=%async_computation.34 | async-start | bytes 2211840 | tf_op jit(solution)/shard_map/all_gather | solution.py:172
  787.4 7.5 collective-permute-start.3
  816.3 62.1 %reduce-scatter.32.cloned.1.call-start = ((), (), s32[]{:S(2)}) async-start(), calls=%async_computation.35 | async-start | bytes 2211840 | tf_op jit(solution)/shard_map/reduce_scatter | solution.py:180
  852.0 176.4 %reduce-scatter.40.cloned.1.call-start = ((), (), s32[]{:S(2)}) async-start(), calls=%async_computation.39 | async-start | bytes 1253376 | tf_op jit(solution)/shard_map/reduce_scatter | solution.py:343
  862.8 24.8 %copy-start.121 = (f32[100,2]{0,1:T(2,128)S(1)}, f32[100,2]{0,1:T(2,128)}, u32[]{:S(2)}) copy-start(f32[100,2]{0,1:T(2,128)} %copy-done.120) | copy-start | bytes 2404
  865.4 166.6 %reduce-scatter.42.cloned.1.call-start = ((), (), s32[]{:S(2)}) async-start(), calls=%async_computation.40 | async-start | bytes 1253376 | tf_op jit(solution)/shard_map/reduce_scatter | solution.py:343
  880.5 16.7 %all-to-all-start.11 = ((bf16[16,2,9,768]{3,1,2,0:T(2,128)(2,1)}), bf16[16,2,9,768]{3,1,2,0:T(2,128)(2,1)}, u32[]{:S(2)}, u32[]{:S(2)}) async-start(bf16[16,2,9,768]{3,1,2,0:T(2,128)(2,1)} %copy.614), calls=%async_computation.17 | async-start | bytes 884736 | tf_op jit(solution)/shard_map/all_to_all | solution.py:183
  887.5 221.2 %reduce-scatter.44.cloned.1.call-start = ((), (), s32[]{:S(2)}) async-start(), calls=%async_computation.41 | async-start | bytes 1253376 | tf_op jit(solution)/shard_map/reduce_scatter | solution.py:343
  911.1 277.3 %reduce-scatter.34.cloned.1.call-start = ((), (), s32[]{:S(2)}) async-start(), calls=%async_computation.36 | async-start | bytes 3760128 | tf_op jit(solution)/shard_map/reduce_scatter | solution.py:340
  918.1 350.3 %reduce-scatter.36.cloned.1.call-start = ((), (), s32[]{:S(2)}) async-start(), calls=%async_computation.37 | async-start | bytes 3760128 | tf_op jit(solution)/shard_map/reduce_scatter | solution.py:340
  922.2 425.9 %reduce-scatter.38.cloned.1.call-start = ((), (), s32[]{:S(2)}) async-start(), calls=%async_computation.38 | async-start | bytes 3760128 | tf_op jit(solution)/shard_map/reduce_scatter | solution.py:340
  991.6 447.2 %all-reduce.18.cloned.1.call-start = ((), (), s32[]{:S(2)}) async-start(), calls=%async_computation.44 | async-start | bytes 331776
  1028.4 451.4 %all-reduce.20.cloned.1.call-start = ((), (), s32[]{:S(2)}) async-start(), calls=%async_computation.45 | async-start | bytes 589824 | tf_op jit(solution)/shard_map/psum | solution.py:354
  (137 other events, 645.6 us)
Sparse Core Ops, SparseCore 0:
  10.2 53.5 all-gather.25
  66.0 40.7 all-gather.27
  126.1 27.5 all-gather.13
  162.3 26.1 reduce-scatter.21
  249.3 32.0 all-gather.15
  290.0 26.1 reduce-scatter.23
  385.5 28.8 all-gather.17
  423.1 26.1 reduce-scatter.25
  498.3 26.8 all-gather.19
  535.2 26.1 reduce-scatter.27
  658.4 25.7 all-gather.21
  694.2 26.1 reduce-scatter.29
  816.4 25.7 all-gather.23
  852.2 26.1 reduce-scatter.31
  881.5 73.7 reduce-scatter.39
  958.3 73.6 reduce-scatter.41
  1035.0 73.6 reduce-scatter.43
  1111.9 76.5 reduce-scatter.33
  1191.9 76.4 reduce-scatter.35
  1271.6 76.4 reduce-scatter.37
  1353.1 85.6 all-reduce.17
  1441.9 37.8 all-reduce.19
where the time goes:
time: 1500 us; the launch traced here: 1490 us
  waiting for transfers between devices  730 us (49%)
  local copies, waits for them, and re-layouts  231 us (15%)
  matrix products  190 us (13%)
  blocking collectives  140 us (9%)
  other arithmetic  127 us (8%)
  starting transfers between devices  54.3 us (4%)
  between operations  18 us (1%)
    reduce_scatter x3, waiting for transfers between devices, shards(): lax.psum_scatter(dense_grads[2].astype(jnp.bfloat16), 'expert', scatter_d...  238 us
    unnamed x23, waiting for transfers between devices  90.5 us
    all_gather x3, waiting for transfers between devices, layer_forward(): lax.all_gather(lax.all_to_all(sending, 'expert', split_axis=0, concat_axi...  88 us
    reduce_scatter x3, waiting for transfers between devices, shards(): lax.psum_scatter(dense_grads[3].astype(jnp.bfloat16), 'expert', scatter_d...  80.2 us
    all_gather x3, waiting for transfers between devices, layer_backward(): grad_all = lax.all_gather(grad_recv, 'replica', axis=0, tiled=True)  66.8 us
    another operation x27, other arithmetic, shards(): saved_all = jax.tree.map(lambda *leaves: jnp.stack(leaves), *saved_list)  44.7 us
    unnamed x353, local copies, waits for them, and re-layouts  40.7 us
    all_to_all x3, blocking collectives, layer_forward(): lax.all_to_all(sending, 'expert', split_axis=0, concat_axis=0, tiled=True)  36 us
  transfers between devices with their start and end apart: 32, of which 29 were waited for; matrix products, arithmetic and copies ran while one was open for 18% of the time, Pallas kernels for 0%

commit v1 on v0

v1 whole, which is shorter than its diff:
```python
import functools
import math

import jax
import jax.numpy as jnp
from jax import lax
from jax.experimental import pallas as pl
from jax.experimental.pallas import tpu as pltpu
from jax.sharding import PartitionSpec as P

D = 768
HEADS = 12
HEAD_DIM = 64
S = 50
EPSILON = 1e-06
PACKED = 3200
BF = jnp.bfloat16
F32 = jnp.float32


def mm(left, right):
    return jnp.dot(left, right, preferred_element_type=F32)


def ein(spec, *args):
    return jnp.einsum(spec, *args, preferred_element_type=F32)


def norm_apply(inputs, gain_vec, bias_vec):
    centre = jnp.mean(inputs, axis=-1, keepdims=True)
    spread = jnp.mean(jnp.square(inputs - centre), axis=-1, keepdims=True)
    return (inputs - centre) * lax.rsqrt(spread + EPSILON) * gain_vec + bias_vec


def gelu_tanh(pre_act):
    return jax.nn.gelu(pre_act, approximate=True)


def handed(value, by):
    length = lax.axis_size("section")
    pairs = [(i, i + by) for i in range(length) if 0 <= i + by < length]
    return lax.ppermute(value, "section", pairs)


def route_tables(routes, experts, groups, capacity, block):
    micro, rows, _ = routes.shape
    local = experts // groups
    share = block // local + 2
    flat = routes.reshape(micro, rows * 2)
    onehot = (flat[:, :, None] == jnp.arange(experts, dtype=jnp.int32)).astype(BF)
    order = jnp.arange(rows * 2, dtype=jnp.int32)
    earlier = (order[None, :] < order[:, None]).astype(BF)
    before = ein("ab,mbe->mae", earlier, onehot)
    slot = jnp.sum(before * onehot.astype(F32), axis=-1).astype(jnp.int32)
    micro_at = jnp.arange(micro, dtype=jnp.int32)[:, None]
    target = (flat // local) * block + (flat % local) * share + micro_at * capacity + slot
    target = target.reshape(micro * rows, 2)
    places = jnp.arange(groups * block, dtype=jnp.int32)[:, None]
    pick_first = (target[None, :, 0] == places).astype(BF)
    pick_second = (target[None, :, 1] == places).astype(BF)
    onehot = onehot.reshape(micro * rows, 2, experts).astype(F32)
    return onehot[:, 0], onehot[:, 1], pick_first, pick_second


MESH = pl.DeviceIdType.MESH
RING = 4


def peer_at(me, step):
    row, column = me // RING, me % RING
    return (row + step // RING) % RING * RING + (column + step % RING) % RING


def origin_at(me, step):
    row, column = me // RING, me % RING
    return (row + RING - step // RING) % RING * RING + (column + RING - step % RING) % RING


def greet(me, partner, across, groups):
    barrier = pltpu.get_barrier_semaphore()

    def one(step, carry):
        pl.semaphore_signal(barrier, inc=1, device_id={"expert": peer_at(me, step)}, device_id_type=MESH)
        return carry

    lax.fori_loop(1, groups, one, 0)
    pl.semaphore_signal(barrier, inc=1, device_id={"replica": partner}, device_id_type=MESH)
    pl.semaphore_signal(barrier, inc=1, device_id={"replica": across}, device_id_type=MESH)
    pl.semaphore_wait(barrier, groups + 1)


def remote(source, target, sems, step, device):
    return pltpu.make_async_remote_copy(
        src_ref=source, dst_ref=target, send_sem=sems[0].at[step], recv_sem=sems[1].at[step],
        device_id=device, device_id_type=MESH,
    )


def spread_kernel(groups, send, out, swap_s, swap_r, near_s, near_r, far_s, far_r, last_s, last_r, own_sem):
    me, rep = lax.axis_index("expert"), lax.axis_index("replica")
    partner = rep + 1 - 2 * (rep % 2)
    across = (rep + 2) % 4
    greet(me, partner, across, groups)

    def swap(step):
        there = peer_at(me, step)
        return remote(send.at[there], out.at[rep, me], (swap_s, swap_r), step, {"expert": there})

    def near(step, block):
        from_at = origin_at(me, step)
        return remote(block, out.at[rep, from_at], (near_s, near_r), step, {"replica": partner})

    def far(step, block):
        from_at = origin_at(me, step)
        return remote(block, out.at[rep, from_at], (far_s, far_r), step, {"replica": across})

    def last(step):
        from_at = origin_at(me, step)
        return remote(out.at[across, from_at], out.at[across, from_at], (last_s, last_r), step, {"replica": partner})

    far(0, send.at[me]).start()
    near(0, send.at[me]).start()
    keep = pltpu.make_async_copy(send.at[me], out.at[rep, me], own_sem)
    keep.start()

    def first(step, carry):
        swap(step).start()
        return carry

    lax.fori_loop(1, groups, first, 0)

    def pass_on(step, carry):
        swap(step).wait_recv()
        block = out.at[rep, origin_at(me, step)]
        far(step, block).start()
        near(step, block).start()
        return carry

    lax.fori_loop(1, groups, pass_on, 0)

    def pass_last(step, carry):
        far(step, send.at[me]).wait_recv()
        last(step).start()
        return carry

    lax.fori_loop(0, groups, pass_last, 0)

    def finish(step, carry):
        near(step, send.at[me]).wait()
        far(step, send.at[me]).wait_send()
        last(step).wait()
        return carry

    lax.fori_loop(0, groups, finish, 0)

    def sent(step, carry):
        swap(step).wait_send()
        return carry

    lax.fori_loop(1, groups, sent, 0)
    keep.wait()


def spread_rows(sending):
    groups, block, _ = sending.shape
    out = pl.pallas_call(
        functools.partial(spread_kernel, groups),
        out_shape=jax.ShapeDtypeStruct((4,) + sending.shape, sending.dtype),
        in_specs=[pl.BlockSpec(memory_space=pltpu.VMEM)],
        out_specs=pl.BlockSpec(memory_space=pl.ANY),
        scratch_shapes=[pltpu.SemaphoreType.DMA((groups,))] * 8 + [pltpu.SemaphoreType.DMA],
        compiler_params=pltpu.CompilerParams(collective_id=0, has_side_effects=True),
        name="spread_rows",
    )(sending)
    return out.reshape(4 * groups, block, D)


def return_kernel(groups, part, out, near_in, far_in, pair, total, near_s, near_r, far_s, far_r, home_s, home_r, own_sem):
    me, rep = lax.axis_index("expert"), lax.axis_index("replica")
    partner = rep + 1 - 2 * (rep % 2)
    across = (rep + 2) % 4
    partner_across = (partner + 2) % 4
    greet(me, partner, across, groups)

    def near(side, step):
        whose = partner_across if side == 0 else partner
        return remote(
            part.at[whose, peer_at(me, step)], near_in.at[side, step],
            (near_s.at[side], near_r.at[side]), step, {"replica": partner},
        )

    def far(step):
        return remote(pair.at[step], far_in.at[step], (far_s, far_r), step, {"replica": across})

    def home(step):
        return remote(total.at[step], out.at[me], (home_s, home_r), step, {"expert": peer_at(me, step)})

    for side in range(2):

        def send_near(step, carry, side=side):
            near(side, step).start()
            return carry

        lax.fori_loop(0, groups, send_near, 0)

    def send_far(step, carry):
        near(0, step).wait_recv()
        both = part[across, peer_at(me, step)].astype(F32) + near_in[0, step].astype(F32)
        pair[step] = both.astype(BF)
        far(step).start()
        return carry

    lax.fori_loop(0, groups, send_far, 0)

    def close(step):
        near(1, step).wait_recv()
        far(step).wait_recv()
        whole = part[rep, peer_at(me, step)].astype(F32) + near_in[1, step].astype(F32) + far_in[step].astype(F32)
        total[step] = whole.astype(BF)

    close(0)
    keep = pltpu.make_async_copy(total.at[0], out.at[me], own_sem)
    keep.start()

    def send_home(step, carry):
        close(step)
        home(step).start()
        return carry

    lax.fori_loop(1, groups, send_home, 0)

    def finish(step, carry):
        home(step).wait()
        return carry

    lax.fori_loop(1, groups, finish, 0)

    def sent(step, carry):
        near(0, step).wait_send()
        near(1, step).wait_send()
        far(step).wait_send()
        return carry

    lax.fori_loop(0, groups, sent, 0)
    keep.wait()


def return_rows(partial_rows):
    sources, block, _ = partial_rows.shape
    groups = sources // 4
    shape = (groups, block, D)
    out = pl.pallas_call(
        functools.partial(return_kernel, groups),
        out_shape=jax.ShapeDtypeStruct(shape, BF),
        in_specs=[pl.BlockSpec(memory_space=pltpu.VMEM)],
        out_specs=pl.BlockSpec(memory_space=pltpu.VMEM),
        scratch_shapes=[
            pltpu.VMEM((2,) + shape, BF), pltpu.VMEM(shape, BF), pltpu.VMEM(shape, BF), pltpu.VMEM(shape, BF),
            pltpu.SemaphoreType.DMA((2, groups)), pltpu.SemaphoreType.DMA((2, groups)),
        ] + [pltpu.SemaphoreType.DMA((groups,))] * 4 + [pltpu.SemaphoreType.DMA],
        compiler_params=pltpu.CompilerParams(collective_id=1, has_side_effects=True),
        name="return_rows",
    )(partial_rows.reshape(4, groups, block, D))
    return out.reshape(groups * block, D)


def by_expert(rows):
    sources, block, _ = rows.shape
    window = 24
    at = jnp.arange(window, dtype=jnp.int32)[None, :, None]
    low = jnp.where(at < block // 2, rows[:, :window], 0)
    high = jnp.where(at >= window - block // 2, rows[:, block - window :], 0)
    return jnp.stack([low, high]).reshape(2, sources * window, D)


def from_expert(windows, block):
    window = 24
    shaped = windows.reshape(2, -1, window, D)
    edge = block - window
    return jnp.concatenate(
        [shaped[0, :, :edge], shaped[0, :, edge:] + shaped[1, :, : window - edge], shaped[1, :, window - edge :]], axis=1
    ).astype(BF)


def attention_inputs(joint, images):
    shaped = joint.reshape(images, S, 3, HEADS, HEAD_DIM)
    return shaped[:, :, 0], shaped[:, :, 1], shaped[:, :, 2]


def layer_forward(dense, experts, tables, tokens):
    gain, bias, attend_w, output_w, router_w = dense
    weight_in, weight_out = experts
    hot_first, hot_second, pick_first, pick_second = tables
    rows = tokens.shape[0]
    images = rows // S
    scaling = 1.0 / math.sqrt(HEAD_DIM)
    groups = lax.axis_size("expert")
    inputs = tokens.astype(F32)
    normed_one = norm_apply(inputs, gain[0], bias[0]).astype(BF)
    joint = mm(normed_one, attend_w).astype(BF)
    queries, keys, values = attention_inputs(joint, images)
    scores = ein("nqhc,nkhc->nhqk", queries, keys) * scaling
    row_max = jnp.max(scores, axis=-1, keepdims=True)
    raised = jnp.exp(scores - row_max)
    row_total = jnp.sum(raised, axis=-1, keepdims=True)
    log_total = row_max + jnp.log(row_total)
    prob = (raised / row_total).astype(BF)
    mixed = ein("nhqk,nkhc->nqhc", prob, values).reshape(rows, D).astype(BF)
    hidden = inputs + mm(mixed, output_w)
    normed_two = norm_apply(hidden, gain[1], bias[1]).astype(BF)
    logits = mm(normed_two, router_w)
    chosen = jnp.stack([jnp.sum(logits * hot_first, -1), jnp.sum(logits * hot_second, -1)], axis=1)
    gates = jax.nn.softmax(chosen, axis=-1)
    sending = mm(pick_first + pick_second, normed_two).astype(BF).reshape(groups, -1, D)
    received = spread_rows(sending)
    shaped = by_expert(received)
    pre_act = ein("esd,edh->esh", shaped, weight_in)
    active = gelu_tanh(pre_act).astype(BF)
    partial = ein("esh,ehd->esd", active, weight_out)
    returned = return_rows(from_expert(partial, received.shape[1]))
    first_rows = ein("pr,pd->rd", pick_first, returned)
    second_rows = ein("pr,pd->rd", pick_second, returned)
    output = hidden + (gates[:, 0:1] * first_rows + gates[:, 1:2] * second_rows)
    stored = dict(
        inputs=inputs, normed_one=normed_one, joint=joint, log_total=log_total, mixed=mixed,
        hidden=hidden, normed_two=normed_two, gates=gates, first_rows=first_rows.astype(BF),
        second_rows=second_rows.astype(BF), received=shaped, pre_act=pre_act, active=active,
    )
    return output, stored


def layer_backward(dense, experts, tables, stored, cotangent):
    gain, bias, attend_w, output_w, router_w = dense
    weight_in, weight_out = experts
    hot_first, hot_second, pick_first, pick_second = tables
    rows = cotangent.shape[0]
    images = rows // S
    scaling = 1.0 / math.sqrt(HEAD_DIM)
    groups = lax.axis_size("expert")
    gates = stored["gates"]
    first_send = (gates[:, 0:1] * cotangent).astype(BF)
    second_send = (gates[:, 1:2] * cotangent).astype(BF)
    grad_send = mm(pick_first, first_send) + mm(pick_second, second_send)
    grad_all = spread_rows(grad_send.astype(BF).reshape(groups, -1, D))
    gate_grad = jnp.stack(
        [
            jnp.sum(cotangent * stored["first_rows"].astype(F32), axis=-1),
            jnp.sum(cotangent * stored["second_rows"].astype(F32), axis=-1),
        ],
        axis=1,
    )
    chosen_grad = gates * (gate_grad - jnp.sum(gates * gate_grad, axis=-1, keepdims=True))
    logit_grad = (chosen_grad[:, 0:1] * hot_first + chosen_grad[:, 1:2] * hot_second).astype(BF)
    router_g = mm(stored["normed_two"].T, logit_grad)
    router_part = mm(logit_grad, router_w.T)
    grad_shaped = by_expert(grad_all)
    act_grad = ein("esd,ehd->esh", grad_shaped, weight_out)
    pre_grad = jax.vjp(gelu_tanh, stored["pre_act"])[1](act_grad)[0].astype(BF)
    back_part = ein("esh,edh->esd", pre_grad, weight_in)
    back_home = return_rows(from_expert(back_part, grad_all.shape[1]))
    both_back = mm((pick_first + pick_second).T, back_home)
    normed_grad = router_part + both_back
    pull_two = jax.vjp(norm_apply, stored["hidden"], gain[1], bias[1])[1]
    hidden_part, gain_two, bias_two = pull_two(normed_grad)
    hidden_grad = cotangent + hidden_part
    hidden_b = hidden_grad.astype(BF)
    output_g = mm(stored["mixed"].T, hidden_b)
    mixed_grad = mm(hidden_b, output_w.T).astype(BF).reshape(images, S, HEADS, HEAD_DIM)
    queries, keys, values = attention_inputs(stored["joint"], images)
    scores = ein("nqhc,nkhc->nhqk", queries, keys) * scaling
    prob = jnp.exp(scores - stored["log_total"])
    value_grad = ein("nhqk,nqhc->nkhc", prob.astype(BF), mixed_grad)
    prob_grad = ein("nqhc,nkhc->nhqk", mixed_grad, values)
    row_delta = jnp.sum(prob * prob_grad, axis=-1, keepdims=True)
    score_grad = (prob * (prob_grad - row_delta) * scaling).astype(BF)
    query_grad = ein("nhqk,nkhc->nqhc", score_grad, keys)
    key_grad = ein("nhqk,nqhc->nkhc", score_grad, queries)
    joint_grad = jnp.concatenate(
        [query_grad.reshape(rows, D), key_grad.reshape(rows, D), value_grad.reshape(rows, D)], axis=1
    ).astype(BF)
    attend_g = mm(stored["normed_one"].T, joint_grad)
    normed_one_grad = mm(joint_grad, attend_w.T)
    pull_one = jax.vjp(norm_apply, stored["inputs"], gain[0], bias[0])[1]
    input_part, gain_one, bias_one = pull_one(normed_one_grad)
    input_grad = hidden_grad + input_part
    dense_grads = (jnp.stack([gain_one, gain_two]), jnp.stack([bias_one, bias_two]), attend_g, output_g, router_g)
    expert_grads = (
        ein("esd,esh->edh", stored["received"], pre_grad),
        ein("esh,esd->ehd", stored["active"], grad_shaped),
    )
    return input_grad, dense_grads, expert_grads


def packed(gain, bias, attend, output, router):
    joined = jnp.concatenate([attend, output, router, gain.T, bias.T], axis=1)
    return jnp.pad(joined, ((0, 0), (0, PACKED - joined.shape[1])))


def unpacked(joined, experts):
    at = [3 * D, 4 * D, 4 * D + experts, 4 * D + experts + 2, 4 * D + experts + 4]
    return (
        joined[:, at[2] : at[3]].T,
        joined[:, at[3] : at[4]].T,
        joined[:, : at[0]],
        joined[:, at[0] : at[1]],
        joined[:, at[1] : at[2]],
    )


def shards(
    boundary, routes, norm_gains, norm_biases, attend_weight, output_weight, router_weight, expert_in, expert_out
):
    section_at = lax.axis_index("section")
    micro = boundary.shape[1]
    rows = boundary.shape[2] * boundary.shape[3]
    own = boundary[0].reshape(micro * rows, D)
    total_experts = router_weight.shape[2]
    groups = lax.axis_size("expert")
    capacity = 9
    block = 40
    tables = route_tables(routes[0].reshape(micro, rows, 2), total_experts, groups, capacity, block)
    experts = (expert_in[0], expert_out[0])
    gathered = lax.all_gather(
        packed(norm_gains[0], norm_biases[0], attend_weight[0], output_weight[0], router_weight[0]),
        "expert", axis=0, tiled=True,
    )
    gain, bias, attend_w, output_w, router_w = unpacked(gathered, total_experts)
    dense = (gain.astype(F32), bias.astype(F32), attend_w, output_w, router_w)

    first_out, _ = layer_forward(dense, experts, tables, own)
    incoming = handed(first_out.astype(BF), 1)
    tokens = jnp.where(section_at == 0, own, incoming)
    final_out, stored = layer_forward(dense, experts, tables, tokens)
    first_back, _, _ = layer_backward(dense, experts, tables, stored, own.astype(F32))
    incoming_back = handed(first_back.astype(BF), -1)
    cotangent = jnp.where(section_at == 1, own, incoming_back).astype(F32)
    input_grad, dense_grads, expert_grads = layer_backward(dense, experts, tables, stored, cotangent)

    mine = packed(*dense_grads).astype(BF)
    owned = lax.psum_scatter(mine, "expert", scatter_dimension=0, tiled=True)
    owned = lax.psum(owned, "replica").astype(F32)
    gain_g, bias_g, attend_g, output_g, router_g = unpacked(owned, total_experts)
    merged = jnp.where(section_at == 0, input_grad.astype(BF), final_out.astype(BF)).reshape(boundary.shape)
    return (
        merged, gain_g[None], bias_g[None], attend_g[None], output_g[None], router_g[None],
        expert_grads[0][None], expert_grads[1][None],
    )


def solution(mesh):
    in_specs = (
        P("section", None, ("expert", "replica"), None, None),
        P("section", None, ("expert", "replica"), None, None),
        P("section", None, "expert"),
        P("section", None, "expert"),
        P("section", "expert", None),
        P("section", "expert", None),
        P("section", "expert", None),
        P("section", "expert", None, "replica"),
        P("section", "expert", "replica", None),
    )
    out_specs = in_specs[:1] + in_specs[2:]
    return jax.shard_map(shards, mesh=mesh, in_specs=in_specs, out_specs=out_specs, check_vma=False)
```

time: 1500 us -> 813 us (0.54)
  waiting for transfers between devices: 730 us -> 161 us
  Pallas kernels: 0 us -> 307 us
  blocking collectives: 140 us -> 0 us
  local copies, waits for them, and re-layouts: 231 us -> 91.8 us
  other arithmetic: 127 us -> 49 us
  starting transfers between devices: 54.3 us -> 6.83 us
    reduce_scatter x12 -> x0, waiting for transfers between devices: 371 us -> none  [the longest x3 238 us: shards(): lax.psum_scatter(dense_grads[2].astype(jnp.bfloat16), 'expert', scatter_d...]
    pallas_call x0 -> x8, Pallas kernels: none -> 307 us  [the longest x4 166 us: return_rows(): pl.pallas_call(functools.partial(return_kernel, groups), out_shape=jax.Sh...]
    all_gather x8 -> x1, waiting for transfers between devices: 180 us -> 51.5 us  [shards(): lax.all_gather(packed(norm_gains[0], norm_biases[0], attend_weight[0], ou...]
    all_to_all x6 -> x0, blocking collectives: 70.7 us -> none  [the longest x3 36 us: layer_forward(): lax.all_to_all(sending, 'expert', split_axis=0, concat_axis=0, tiled=True)]
    all_gather x3 -> x0, blocking collectives: 61.9 us -> none  [the longest x1 21.8 us: gather_dense(): lax.all_gather(norm_biases[0], 'expert', axis=1, tiled=True)]
    reshape x54 -> x11, local copies, waits for them, and re-layouts: 83.3 us -> 28.7 us  [the longest x2 8.21 us: attention_inputs(): shaped = joint.reshape(images, S, 3, HEADS, HEAD_DIM)]
    another operation x45 -> x10, other arithmetic: 57.2 us -> 13.6 us  [the longest x27 44.7 us: shards(): saved_all = jax.tree.map(lambda *leaves: jnp.stack(leaves), *saved_list)]
    all_to_all x6 -> x0, waiting for transfers between devices: 43.2 us -> none  [the longest x3 25.8 us: layer_forward(): lax.all_to_all(produced, 'expert', split_axis=0, concat_axis=0, tiled=True)]
  transfers between devices with their start and end apart: 32 -> 5, of which waited for: 29 -> 5; matrix products, arithmetic and copies ran while one was open for 18% -> 4% of each run, Pallas kernels for 0% -> 0%
where the time goes in v1:
time: 813 us; the launch traced here: 807 us
  Pallas kernels  307 us (38%)
  matrix products  176 us (22%)
  waiting for transfers between devices  161 us (20%)
  local copies, waits for them, and re-layouts  91.8 us (11%)
  other arithmetic  49 us (6%)
  between operations  15.2 us (2%)
    pallas_call x4, Pallas kernels, return_rows(): pl.pallas_call(functools.partial(return_kernel, groups), out_shape=jax.Sh...  166 us
    pallas_call x4, Pallas kernels, spread_rows(): pl.pallas_call(functools.partial(spread_kernel, groups), out_shape=jax.Sh...  141 us
    dot_general x25, matrix products, ein(): return jnp.einsum(spec, *args, preferred_element_type=F32)  128 us
    unnamed x4, waiting for transfers between devices  58.3 us
    all_gather x1, waiting for transfers between devices, shards(): lax.all_gather(packed(norm_gains[0], norm_biases[0], attend_weight[0], ou...  51.5 us
    dot_general x23, matrix products, mm(): return jnp.dot(left, right, preferred_element_type=F32)  46 us
    psum x1, waiting for transfers between devices, shards(): owned = lax.psum(owned, 'replica').astype(F32)  36.3 us
  transfers between devices with their start and end apart: 5, of which 5 were waited for; matrix products, arithmetic and copies ran while one was open for 4% of the time, Pallas kernels for 0%

profile of v1, /device:TPU:1, one launch (start us, length us, event | category | flops | bytes accessed | tf_op | source)
XLA Modules:
  0.0 806.5 jit_solution(18150293108680012284)
XLA Ops:
  18.1 51.5 %all-gather.2.cloned.1.call-done = bf16[768,3200]{1,0:T(8,128)(2,1)} async-done(((bf16[48,3200]{1,0:T(8,128)(2,1)}), bf16[768,3200]{1,0:T(8,128)(2,1)}) %all-gather.2.cloned.1.call-update) | async-done | bytes 4915216 | tf_op jit(solution)/shard_map/all_gather | solution.py:423
  71.5 3.9 convolution_convert_fusion.2
  75.4 4.2 reshape.385
  79.6 3.3 fusion.278
  82.9 2.3 fusion.284
  85.2 3.0 convolution_multiply_fusion.1
  88.2 3.5 fusion.86
  91.8 2.1 copy.137
  99.8 34.4 %spread_rows.4 = bf16[4,16,40,768]{3,2,1,0:T(8,128)(2,1)} custom-call(bf16[16,40,768]{2,1,0:T(8,128)(2,1)} %bitcast.260), custom_call_target="tpu_custom_call" | custom-call | tf_op jit(solution)/shard_map/spread_rows/pallas_call | solution.py:166
  134.3 5.0 slice_select_fusion.7
  139.2 12.4 %fusion.15 = f32[2,1536,768]{2,1,0:T(8,128)} fusion(bf16[1,1536,768]{2,1,0:T(8,128)(2,1)} %bitcast.255, bf16[1,1536,768]{2,1,0:T(8,128)(2,1)} %bitcast.254, bf16[1,2,768,768]{3,2,1,0:T(8,128)(2,1)S(1)} %copy-done, bf16[1,2,768,768]{3,2,1,0:T(8,128)(2,1)} %param.16), kind=kOutput, calls=%fused_computation.24 | convolution fusion | flops 7271350272 | bytes 18874368 | tf_op jit(solution)/shard_map/esh,ehd->esd/dot_general | solution.py:26
  153.7 4.1 convert.111
  161.4 38.6 %return_rows.4 = bf16[16,40,768]{2,1,0:T(8,128)(2,1)} custom-call(bf16[4,16,40,768]{3,2,1,0:T(8,128)(2,1)} %pad_maximum_fusion.2.part), custom_call_target="tpu_custom_call" | custom-call | tf_op jit(solution)/shard_map/return_rows/pallas_call | solution.py:252
  203.5 5.1 collective-permute-start
  208.7 4.9 collective-permute-done
  214.0 3.9 convolution_convert_fusion.1
  217.9 4.0 reshape.390
  227.0 2.4 convert_element_type.241
  233.8 34.9 %spread_rows.5 = bf16[4,16,40,768]{3,2,1,0:T(8,128)(2,1)} custom-call(bf16[16,40,768]{2,1,0:T(8,128)(2,1)} %bitcast.261), custom_call_target="tpu_custom_call" | custom-call | tf_op jit(solution)/shard_map/spread_rows/pallas_call | solution.py:166
  268.7 2.9 slice_select_fusion.5
  271.8 7.0 fusion.38
  278.9 8.3 %fusion.45 = f32[2,1536,768]{2,1,0:T(8,128)S(1)} fusion(bf16[1,2,768,768]{3,2,1,0:T(8,128)(2,1)S(1)} %copy-done, f32[2,1536,768]{2,1,0:T(8,128)} %fusion.38), kind=kOutput, calls=%fused_computation.60 | convolution fusion | flops 3645112320 | bytes 21233664 | tf_op jit(solution)/shard_map/esh,ehd->esd/dot_general | solution.py:26
  290.1 45.3 %return_rows.5 = bf16[16,40,768]{2,1,0:T(8,128)(2,1)} custom-call(bf16[4,16,40,768]{3,2,1,0:T(8,128)(2,1)} %pad_maximum_fusion.3.part), custom_call_target="tpu_custom_call" | custom-call | tf_op jit(solution)/shard_map/return_rows/pallas_call | solution.py:252
  337.1 2.9 fusion.168
  343.3 35.3 %spread_rows.6 = bf16[4,16,40,768]{3,2,1,0:T(8,128)(2,1)} custom-call(bf16[16,40,768]{2,1,0:T(8,128)(2,1)} %bitcast.240), custom_call_target="tpu_custom_call" | custom-call | tf_op jit(solution)/shard_map/spread_rows/pallas_call | solution.py:166
  378.6 5.0 slice_select_fusion.3
  383.5 15.7 %fusion.40 = f32[2,1536,768]{2,1,0:T(8,128)} fusion(f32[2,1536,768]{2,1,0:T(8,128)} %fusion.38, bf16[1,1536,768]{2,1,0:T(8,128)(2,1)} %bitcast.257, bf16[1,1536,768]{2,1,0:T(8,128)(2,1)} %bitcast.256, bf16[1,2,768,768]{3,2,1,0:T(8,128)(2,1)S(1)} %copy-done, bf16[1,2,768,768]{3,2,1,0:T(8,128)(2,1)} %param.16), kind=kOutput, calls=%fused_computation.49 | convolution fusion | flops 7297302528 | bytes 28311552 | tf_op jit(solution)/shard_map/esh,edh->esd/dot_general | solution.py:26
  401.2 4.1 convert.115
  407.7 39.3 %return_rows.6 = bf16[16,40,768]{2,1,0:T(8,128)(2,1)} custom-call(bf16[4,16,40,768]{3,2,1,0:T(8,128)(2,1)} %pad_maximum_fusion.4.part), custom_call_target="tpu_custom_call" | custom-call | tf_op jit(solution)/shard_map/return_rows/pallas_call | solution.py:252
  451.0 2.6 convolution_convert_fusion.15
  453.6 2.5 reshape.399
  456.1 3.2 fusion.176
  460.7 4.9 fusion.90
  465.5 5.0 fusion.93
  472.6 2.4 reshape.402
  477.1 2.4 reshape.401
  479.5 2.1 copy.148
  481.6 2.4 reshape.400
  484.0 3.8 multiply_reduce_fusion.10
  490.5 10.1 %collective-permute-done.1 = bf16[200,768]{1,0:T(8,128)(2,1)} collective-permute-done((bf16[200,768]{1,0:T(8,128)(2,1)}, bf16[200,768]{1,0:T(8,128)(2,1)}, u32[]{:S(2)}, u32[]{:S(2)}) %collective-permute-start.1) | collective-permute-done | bytes 307232 | tf_op jit(solution)/shard_map/ppermute | solution.py:42
  504.1 36.6 %spread_rows.7 = bf16[4,16,40,768]{3,2,1,0:T(8,128)(2,1)} custom-call(bf16[16,40,768]{2,1,0:T(8,128)(2,1)} %bitcast.241), custom_call_target="tpu_custom_call" | custom-call | tf_op jit(solution)/shard_map/spread_rows/pallas_call | solution.py:166
  540.7 2.8 slice_select_fusion.1
  543.5 13.6 %add_convert_fusion = bf16[2,1536,768]{2,1,0:T(8,128)(2,1)} fusion(f32[2,1536,768]{2,1,0:T(8,128)} %fusion.38, bf16[1,1536,768]{2,1,0:T(8,128)(2,1)S(1)} %bitcast.252, bf16[1,1536,768]{2,1,0:T(8,128)(2,1)S(1)} %bitcast.250, bf16[1,2,768,768]{3,2,1,0:T(8,128)(2,1)S(1)} %copy-done), kind=kOutput, calls=%fused_computation.18 | convolution fusion | flops 3673423872 | bytes 21233664 | tf_op jit(solution)/shard_map/esd,ehd->esh/dot_general | solution.py:26
  557.2 5.9 fusion.48
  566.7 42.4 %return_rows.7 = bf16[16,40,768]{2,1,0:T(8,128)(2,1)} custom-call(bf16[4,16,40,768]{3,2,1,0:T(8,128)(2,1)} %pad_maximum_fusion.5.part), custom_call_target="tpu_custom_call" | custom-call | tf_op jit(solution)/shard_map/return_rows/pallas_call | solution.py:252
  613.6 2.5 convolution_convert_fusion.14
  616.2 2.6 reshape.407
  618.9 3.2 fusion.173
  623.4 4.7 fusion.96
  628.1 4.7 fusion.99
  632.9 2.7 convolution_convert_fusion.3
  636.4 2.1 copy.155
  638.5 2.4 reshape.409
  643.0 2.4 reshape.408
  647.5 2.4 reshape.410
  652.9 3.1 convolution_convert_fusion
  656.0 4.1 fusion.154
  661.2 8.4 %concatenate.70 = bf16[768,3108]{1,0:T(8,128)(2,1)} concatenate(bf16[768,2304]{1,0:T(8,128)(2,1)} %convolution_convert_fusion, bf16[768,768]{1,0:T(8,128)(2,1)} %convolution_convert_fusion.3, bf16[768,32]{1,0:T(8,128)(2,1)} %copy.161, bf16[768,2]{1,0:T(8,128)(2,1)} %bitcast.263, bf16[768,2]{1,0:T(8,128)(2,1)S(1)} %bitcast.262), dimensions={1} | concatenate | bytes 9547776 | tf_op jit(solution)/shard_map/concatenate | solution.py:395
  669.7 4.9 pad.10
  675.2 10.2 %fusion.54 = f32[1,2,768,768]{3,2,1,0:T(8,128)} fusion(bf16[2,1536,768]{2,1,0:T(8,128)(2,1)} %add_convert_fusion, bf16[1,1536,768]{2,1,0:T(8,128)(2,1)} %bitcast.249, bf16[1,1536,768]{2,1,0:T(8,128)(2,1)} %bitcast.247), kind=kOutput, calls=%fused_computation.68 | convolution fusion | flops 3626237952 | bytes 14155776 | tf_op jit(solution)/shard_map/esd,esh->edh/dot_general | solution.py:26
  685.4 10.2 %fusion.55 = f32[1,2,768,768]{3,2,1,0:T(8,128)} fusion(bf16[1,1536,768]{2,1,0:T(8,128)(2,1)S(1)} %bitcast.253, bf16[1,1536,768]{2,1,0:T(8,128)(2,1)S(1)} %bitcast.251, f32[2,1536,768]{2,1,0:T(8,128)} %fusion.38), kind=kOutput, calls=%fused_computation.69 | convolution fusion | flops 3647471616 | bytes 18874368 | tf_op jit(solution)/shard_map/esh,esd->ehd/dot_general | solution.py:26
  695.7 58.2 %reduce-scatter.4.cloned.1.call-done = bf16[48,3200]{1,0:T(8,128)(2,1)} async-done(((bf16[768,3200]{1,0:T(8,128)(2,1)}), bf16[48,3200]{1,0:T(8,128)(2,1)}) %reduce-scatter.4.cloned.1.call-update) | async-done | bytes 307216
  753.9 2.7 fusion.203
  758.6 36.3 %all-reduce.5.cloned.1.call-done = bf16[48,3200]{1,0:T(8,128)(2,1)} async-done(((bf16[48,3200]{1,0:T(8,128)(2,1)}), bf16[48,3200]{1,0:T(8,128)(2,1)}) %all-reduce.5.cloned.1.call-update) | async-done | bytes 307216 | tf_op jit(solution)/shard_map/psum | solution.py:441
  (211 shorter events, 91.4 us)
Async XLA Ops:
  7.2 132.0 %copy-start = (bf16[1,2,768,768]{3,2,1,0:T(8,128)(2,1)S(1)}, bf16[1,2,768,768]{3,2,1,0:T(8,128)(2,1)}, u32[]{:S(2)}) copy-start(bf16[1,2,768,768]{3,2,1,0:T(8,128)(2,1)} %param.17) | copy-start | bytes 7077892
  7.2 7.9 copy-start.18
  7.2 62.4 %all-gather.2.cloned.1.call-start = ((), (), s32[]{:S(2)}) async-start(), calls=%async_computation.1 | async-start | bytes 5222400 | tf_op jit(solution)/shard_map/all_gather | solution.py:423
  11.6 742.3 %reduce-scatter.4.cloned.1.call-start = ((), (), s32[]{:S(2)}) async-start(), calls=%async_computation.3 | async-start | bytes 5222400
  18.0 195.6 %copy-start.4 = (bf16[200,768]{1,0:T(8,128)(2,1)}, bf16[200,768]{1,0:T(8,128)(2,1)S(1)}, u32[]{:S(2)}) copy-start(bf16[200,768]{1,0:T(8,128)(2,1)S(1)} %reshape_squeeze.3) | copy-start | bytes 921604
  97.4 0.8 copy-start.13
  203.5 10.1 %collective-permute-start = (bf16[200,768]{1,0:T(8,128)(2,1)S(1)}, bf16[200,768]{1,0:T(8,128)(2,1)S(1)}, u32[]{:S(2)}, u32[]{:S(2)}) collective-permute-start(bf16[200,768]{1,0:T(8,128)(2,1)S(1)} %fusion.108), channel_id=1, source_target_pairs={{0,64},{1,65},{2,66},{3,67},{4,68},{5,69},{6,70},{7,71},{8,72},{9,... | collective-permute-start | bytes 921608 | tf_op jit(solution)/shard_map/ppermute | solution.py:42
  224.1 1.5 copy-start.10
  224.1 1.5 copy-start.16
  224.1 1.5 copy-start.17
  224.7 1.3 copy-start.1
  231.7 0.7 copy-start.19
  268.7 3.1 copy-start.30
  271.6 7.2 copy-start.24
  271.7 7.2 copy-start.25
  335.4 4.6 copy-start.20
  335.4 5.9 copy-start.5
  337.1 4.7 copy-start.8
  447.0 4.0 copy-start.6
  450.2 0.8 copy-start.22
  456.1 3.2 copy-start.2
  456.1 3.2 copy-start.12
  484.0 4.0 copy-start.7
  484.0 4.1 copy-start.23
  489.2 11.4 %collective-permute-start.1 = (bf16[200,768]{1,0:T(8,128)(2,1)}, bf16[200,768]{1,0:T(8,128)(2,1)}, u32[]{:S(2)}, u32[]{:S(2)}) collective-permute-start(bf16[200,768]{1,0:T(8,128)(2,1)} %fusion.151), channel_id=1, source_target_pairs={{64,0},{65,1},{66,2},{67,3},{68,4},{69,5},{70,6},{71,7},{72,8},{73... | collective-permute-start | bytes 921608 | tf_op jit(solution)/shard_map/ppermute | solution.py:42
  502.1 2.0 copy-start.14
  543.5 13.7 %copy-start.26 = (bf16[64,24,768]{2,1,0:T(8,128)(2,1)}, bf16[64,24,768]{2,1,0:T(8,128)(2,1)S(1)}, u32[]{:S(2)}) copy-start(bf16[64,24,768]{2,1,0:T(8,128)(2,1)S(1)} %get-tuple-element.83) | copy-start | bytes 7077892
  543.5 13.7 %copy-start.28 = (bf16[64,24,768]{2,1,0:T(8,128)(2,1)}, bf16[64,24,768]{2,1,0:T(8,128)(2,1)S(1)}, u32[]{:S(2)}) copy-start(bf16[64,24,768]{2,1,0:T(8,128)(2,1)S(1)} %get-tuple-element.84) | copy-start | bytes 7077892
  543.5 13.7 %copy-start.31 = (bf16[1,2,768,768]{3,2,1,0:T(8,128)(2,1)S(1)}, bf16[1,2,768,768]{3,2,1,0:T(8,128)(2,1)}, u32[]{:S(2)}) copy-start(bf16[1,2,768,768]{3,2,1,0:T(8,128)(2,1)} %param.16) | copy-start | bytes 7077892
  563.2 1.0 copy-start.21
  609.1 3.5 copy-start.15
  612.8 0.8 copy-start.9
  618.8 3.2 copy-start.3
  618.9 3.2 copy-start.11
  674.6 120.3 %all-reduce.5.cloned.1.call-start = ((), (), s32[]{:S(2)}) async-start(), calls=%async_computation.2 | async-start | bytes 614400 | tf_op jit(solution)/shard_map/psum | solution.py:441
  675.2 10.2 %copy-start.27 = (bf16[64,24,768]{2,1,0:T(8,128)(2,1)S(1)}, bf16[64,24,768]{2,1,0:T(8,128)(2,1)}, u32[]{:S(2)}) copy-start(bf16[64,24,768]{2,1,0:T(8,128)(2,1)} %copy-done.26) | copy-start | bytes 7077892
  675.2 10.2 %copy-start.29 = (bf16[64,24,768]{2,1,0:T(8,128)(2,1)S(1)}, bf16[64,24,768]{2,1,0:T(8,128)(2,1)}, u32[]{:S(2)}) copy-start(bf16[64,24,768]{2,1,0:T(8,128)(2,1)} %copy-done.28) | copy-start | bytes 7077892
Sparse Core Ops, SparseCore 0:
  11.7 57.8 all-gather.1
  674.7 79.1 reduce-scatter.3
  756.4 38.5 all-reduce.4

commit v2 on v1

--- a/solution.py
+++ b/solution.py
@@ -13,7 +13,6 @@
 HEAD_DIM = 64
 S = 50
 EPSILON = 1e-06
-PACKED = 3200
 BF = jnp.bfloat16
 F32 = jnp.float32
 
@@ -391,19 +390,217 @@
     return input_grad, dense_grads, expert_grads
 
 
+def along(half, me, first, second):
+    row, column = me // RING, me % RING
+    down, over = (first, second) if half == 0 else (second, first)
+    return (row + down + RING) % RING * RING + (column + over + RING) % RING
+
+
+def greet_lines(me, others):
+    barrier = pltpu.get_barrier_semaphore()
+    for step in range(1, RING):
+        for half in range(2):
+            pl.semaphore_signal(barrier, inc=1, device_id={"expert": along(half, me, step, 0)}, device_id_type=MESH)
+    for other in others:
+        pl.semaphore_signal(barrier, inc=1, device_id={"replica": other}, device_id_type=MESH)
+    pl.semaphore_wait(barrier, 2 * (RING - 1) + len(others))
+
+
+def gather_kernel(mine, out, hop_s, hop_r, near_s, near_r, own_sem):
+    me, rep = lax.axis_index("expert"), lax.axis_index("replica")
+    core = rep % 2
+    partner = rep + 1 - 2 * core
+    greet_lines(me, (partner,))
+
+    def hop(half, first, second):
+        index = first * RING + second
+        from_at = along(half, me, 0, -second) if first else me
+        source = mine.at[half, core] if from_at is me or second == 0 else out.at[half, from_at, core]
+        there = along(half, me, first, 0) if first else along(half, me, 0, second)
+        return remote(source, out.at[half, from_at, core], (hop_s.at[half], hop_r.at[half]), index, {"expert": there})
+
+    def near(half, first, second):
+        block = out.at[half, along(half, me, -first, -second), core]
+        return remote(block, block, (near_s.at[half], near_r.at[half]), first * RING + second, {"replica": partner})
+
+    keep = [pltpu.make_async_copy(mine.at[half], out.at[half, me], own_sem.at[half]) for half in range(2)]
+    for half in range(2):
+        for second in range(1, RING):
+            hop(half, 0, second).start()
+    for half in range(2):
+        keep[half].start()
+        for first in range(1, RING):
+            hop(half, first, 0).start()
+    for second in range(1, RING):
+        for half in range(2):
+            hop(half, 0, second).wait_recv()
+            for first in range(1, RING):
+                hop(half, first, second).start()
+            near(half, 0, second).start()
+    for second in range(RING):
+        for first in range(1, RING):
+            for half in range(2):
+                hop(half, first, second).wait_recv()
+                near(half, first, second).start()
+    for half in range(2):
+        keep[half].wait()
+        for index in range(1, RING * RING):
+            hop(half, index // RING, index % RING).wait_send()
+            near(half, index // RING, index % RING).wait()
+
+
+def gather_dense(mine):
+    halves, rows, columns = mine.shape
+    groups = RING * RING
+    sems = [pltpu.SemaphoreType.DMA((halves, groups))] * 4 + [pltpu.SemaphoreType.DMA((halves,))]
+    out = pl.pallas_call(
+        gather_kernel,
+        out_shape=jax.ShapeDtypeStruct((halves, groups, 2, rows // 2, columns), BF),
+        in_specs=[pl.BlockSpec(memory_space=pltpu.VMEM)],
+        out_specs=pl.BlockSpec(memory_space=pl.ANY),
+        scratch_shapes=sems,
+        compiler_params=pltpu.CompilerParams(collective_id=2, has_side_effects=True),
+        name="gather_dense",
+    )(mine.reshape(halves, 2, rows // 2, columns))
+    return out.reshape(halves, groups * rows, columns)
+
+
+def reduce_kernel(
+    part, out, near_in, pair, one_in, one, two_in, mine, far_in, total, last_in,
+    near_s, near_r, one_s, one_r, two_s, two_r, far_s, far_r, last_s, last_r,
+):
+    me, rep = lax.axis_index("expert"), lax.axis_index("replica")
+    core = rep % 2
+    partner = rep + 1 - 2 * core
+    across = (rep + 2) % 4
+    greet_lines(me, (partner, across))
+
+    def near(half, index):
+        there = along(half, me, index // RING, index % RING)
+        return remote(
+            part.at[half, there, 1 - core], near_in.at[half, index],
+            (near_s.at[half], near_r.at[half]), index, {"replica": partner},
+        )
+
+    def stage_one(half, first):
+        return remote(
+            pair.at[half, pl.ds(first * RING, RING)], one_in.at[half, first - 1],
+            (one_s.at[half], one_r.at[half]), first - 1, {"expert": along(half, me, first, 0)},
+        )
+
+    def stage_two(half, second):
+        return remote(
+            one.at[half, second], two_in.at[half, second - 1],
+            (two_s.at[half], two_r.at[half]), second - 1, {"expert": along(half, me, 0, second)},
+        )
+
+    far = [remote(mine.at[half], far_in.at[half], (far_s, far_r), half, {"replica": across}) for half in range(2)]
+    last = [remote(total.at[half], last_in.at[half], (last_s, last_r), half, {"replica": partner}) for half in range(2)]
+    order = (1, 2, 3, 0)
+
+    for first in order:
+        for half in range(2):
+
+            def send_near(second, carry, half=half, first=first):
+                near(half, first * RING + second).start()
+                return carry
+
+            lax.fori_loop(0, RING, send_near, 0)
+    for first in order:
+        for half in range(2):
+
+            def add_pair(second, carry, half=half, first=first):
+                index = first * RING + second
+                near(half, index).wait_recv()
+                there = along(half, me, first, second)
+                both = part[half, there, core].astype(F32) + near_in[half, index].astype(F32)
+                pair[half, index] = both.astype(BF)
+                return carry
+
+            lax.fori_loop(0, RING, add_pair, 0)
+            if first:
+                stage_one(half, first).start()
+    for half in range(2):
+        for first in range(1, RING):
+            stage_one(half, first).wait_recv()
+
+        def add_one(second, carry, half=half):
+            whole = pair[half, second].astype(F32)
+            for first in range(1, RING):
+                whole = whole + one_in[half, first - 1, second].astype(F32)
+            one[half, second] = whole.astype(BF)
+            return carry
+
+        lax.fori_loop(0, RING, add_one, 0)
+        for second in range(1, RING):
+            stage_two(half, second).start()
+    for half in range(2):
+        whole = one[half, 0].astype(F32)
+        for second in range(1, RING):
+            stage_two(half, second).wait_recv()
+            whole = whole + two_in[half, second - 1].astype(F32)
+        mine[half] = whole.astype(BF)
+        far[half].start()
+    for half in range(2):
+        far[half].wait_recv()
+        total[half] = (mine[half].astype(F32) + far_in[half].astype(F32)).astype(BF)
+        last[half].start()
+        out[half, core] = total[half].astype(F32)
+    for half in range(2):
+        last[half].wait_recv()
+        out[half, 1 - core] = last_in[half].astype(F32)
+        last[half].wait_send()
+        far[half].wait_send()
+        for step in range(1, RING):
+            stage_one(half, step).wait_send()
+            stage_two(half, step).wait_send()
+
+        def sent(index, carry, half=half):
+            near(half, index).wait_send()
+            return carry
+
+        lax.fori_loop(0, RING * RING, sent, 0)
+
+
+def reduce_dense(part):
+    halves, depth, columns = part.shape
+    groups = RING * RING
+    rows = depth // groups // 2
+    block = (rows, columns)
+    out = pl.pallas_call(
+        reduce_kernel,
+        out_shape=jax.ShapeDtypeStruct((halves, 2) + block, F32),
+        in_specs=[pl.BlockSpec(memory_space=pltpu.VMEM)],
+        out_specs=pl.BlockSpec(memory_space=pltpu.VMEM),
+        scratch_shapes=[
+            pltpu.VMEM((halves, groups) + block, BF), pltpu.VMEM((halves, groups) + block, BF),
+            pltpu.VMEM((halves, RING - 1, RING) + block, BF), pltpu.VMEM((halves, RING) + block, BF),
+            pltpu.VMEM((halves, RING - 1) + block, BF), pltpu.VMEM((halves,) + block, BF),
+            pltpu.VMEM((halves,) + block, BF), pltpu.VMEM((halves,) + block, BF), pltpu.VMEM((halves,) + block, BF),
+        ] + [pltpu.SemaphoreType.DMA((halves, groups))] * 2 + [pltpu.SemaphoreType.DMA((halves, RING - 1))] * 4
+        + [pltpu.SemaphoreType.DMA((halves,))] * 4,
+        compiler_params=pltpu.CompilerParams(collective_id=3, has_side_effects=True),
+        name="reduce_dense",
+    )(part.reshape((halves, groups, 2) + block))
+    return out.reshape(halves, 2 * rows, columns)
+
+
 def packed(gain, bias, attend, output, router):
-    joined = jnp.concatenate([attend, output, router, gain.T, bias.T], axis=1)
-    return jnp.pad(joined, ((0, 0), (0, PACKED - joined.shape[1])))
+    edge = 2 * D
+    low = jnp.concatenate([attend[:, :edge], router, gain.T, bias.T], axis=1)
+    high = jnp.concatenate([attend[:, edge:], output], axis=1)
+    return jnp.stack([jnp.pad(side, ((0, 0), (0, edge + 128 - side.shape[1]))) for side in (low, high)])
 
 
 def unpacked(joined, experts):
-    at = [3 * D, 4 * D, 4 * D + experts, 4 * D + experts + 2, 4 * D + experts + 4]
+    low, high = joined[0], joined[1]
+    at = 2 * D + experts
     return (
-        joined[:, at[2] : at[3]].T,
-        joined[:, at[3] : at[4]].T,
-        joined[:, : at[0]],
-        joined[:, at[0] : at[1]],
-        joined[:, at[1] : at[2]],
+        low[:, at : at + 2].T,
+        low[:, at + 2 : at + 4].T,
+        jnp.concatenate([low[:, : 2 * D], high[:, :D]], axis=1),
+        high[:, D : 2 * D],
+        low[:, 2 * D : at],
     )
 
 
@@ -420,9 +617,8 @@
     block = 40
     tables = route_tables(routes[0].reshape(micro, rows, 2), total_experts, groups, capacity, block)
     experts = (expert_in[0], expert_out[0])
-    gathered = lax.all_gather(
-        packed(norm_gains[0], norm_biases[0], attend_weight[0], output_weight[0], router_weight[0]),
-        "expert", axis=0, tiled=True,
+    gathered = gather_dense(
+        packed(norm_gains[0], norm_biases[0], attend_weight[0], output_weight[0], router_weight[0])
     )
     gain, bias, attend_w, output_w, router_w = unpacked(gathered, total_experts)
     dense = (gain.astype(F32), bias.astype(F32), attend_w, output_w, router_w)
@@ -436,9 +632,7 @@
     cotangent = jnp.where(section_at == 1, own, incoming_back).astype(F32)
     input_grad, dense_grads, expert_grads = layer_backward(dense, experts, tables, stored, cotangent)
 
-    mine = packed(*dense_grads).astype(BF)
-    owned = lax.psum_scatter(mine, "expert", scatter_dimension=0, tiled=True)
-    owned = lax.psum(owned, "replica").astype(F32)
+    owned = reduce_dense(packed(*[grad.astype(BF) for grad in dense_grads]))
     gain_g, bias_g, attend_g, output_g, router_g = unpacked(owned, total_experts)
     merged = jnp.where(section_at == 0, input_grad.astype(BF), final_out.astype(BF)).reshape(boundary.shape)
     return (

time: 813 us -> 727 us (0.89)
  waiting for transfers between devices: 161 us -> 15.3 us
  Pallas kernels: 307 us -> 374 us
  between operations: 15.2 us -> 1.87 us
  local copies, waits for them, and re-layouts: 91.8 us -> 101 us
  matrix products: 176 us -> 167 us
    pallas_call x0 -> x2, Pallas kernels: none -> 68.7 us  [the longest x1 38.6 us: reduce_dense(): pl.pallas_call(reduce_kernel, out_shape=jax.ShapeDtypeStruct((halves, 2)...]
    unnamed x4 -> x0, waiting for transfers between devices: 58.3 us -> none
    all_gather x1 -> x0, waiting for transfers between devices: 51.5 us -> none  [shards(): lax.all_gather(packed(norm_gains[0], norm_biases[0], attend_weight[0], ou...]
    psum x1 -> x0, waiting for transfers between devices: 36.3 us -> none  [shards(): owned = lax.psum(owned, 'replica').astype(F32)]
    slice x0 -> x10, local copies, waits for them, and re-layouts: none -> 14.7 us  [the longest x2 6.26 us: unpacked(): low, high = (joined[0], joined[1])]
    another operation x8 -> x10, other arithmetic: 13.5 us -> 17.1 us
  transfers between devices with their start and end apart: 5 -> 2, of which waited for: 5 -> 2; matrix products, arithmetic and copies ran while one was open for 4% -> 0% of each run, Pallas kernels for 0% -> 0%
where the time goes in v2:
time: 727 us; the launch traced here: 720 us
  Pallas kernels  374 us (51%)
  matrix products  167 us (23%)
  local copies, waits for them, and re-layouts  101 us (14%)
  other arithmetic  55.9 us (8%)
  waiting for transfers between devices  15.3 us (2%)
    pallas_call x4, Pallas kernels, return_rows(): pl.pallas_call(functools.partial(return_kernel, groups), out_shape=jax.Sh...  166 us
    pallas_call x4, Pallas kernels, spread_rows(): pl.pallas_call(functools.partial(spread_kernel, groups), out_shape=jax.Sh...  139 us
    dot_general x25, matrix products, ein(): return jnp.einsum(spec, *args, preferred_element_type=F32)  122 us
    dot_general x23, matrix products, mm(): return jnp.dot(left, right, preferred_element_type=F32)  42.4 us
    pallas_call x1, Pallas kernels, reduce_dense(): pl.pallas_call(reduce_kernel, out_shape=jax.ShapeDtypeStruct((halves, 2)...  38.6 us
    pallas_call x1, Pallas kernels, gather_dense(): pl.pallas_call(gather_kernel, out_shape=jax.ShapeDtypeStruct((halves, gro...  30 us
    select_n x4, other arithmetic, by_expert(): low = jnp.where(at < block // 2, rows[:, :window], 0)  15.6 us
    ppermute x2, waiting for transfers between devices, handed(): return lax.ppermute(value, 'section', pairs)  15.3 us
  transfers between devices with their start and end apart: 2, of which 2 were waited for; matrix products, arithmetic and copies ran while one was open for 0% of the time, Pallas kernels for 0%

profile of v2, /device:TPU:1, one launch (start us, length us, event | category | flops | bytes accessed | tf_op | source)
XLA Modules:
  0.0 720.3 jit_solution(12152708629540422625)
XLA Ops:
  12.9 30.0 %gather_dense.1 = bf16[2,16,2,24,1664]{4,3,2,1,0:T(8,128)(2,1)} custom-call(bf16[2,2,24,1664]{3,2,1,0:T(8,128)(2,1)} %pad_maximum_fusion.18.mine), custom_call_target="tpu_custom_call" | custom-call | tf_op jit(solution)/shard_map/gather_dense/pallas_call | solution.py:456
  42.9 4.3 fusion.271
  58.8 4.2 reshape.405
  63.0 3.3 fusion.277
  66.3 2.3 fusion.284
  68.6 3.0 convolution_multiply_fusion.1
  72.5 3.6 fusion.83
  76.0 2.1 copy.143
  84.1 32.5 %spread_rows.4 = bf16[4,16,40,768]{3,2,1,0:T(8,128)(2,1)} custom-call(bf16[16,40,768]{2,1,0:T(8,128)(2,1)} %bitcast.281), custom_call_target="tpu_custom_call" | custom-call | tf_op jit(solution)/shard_map/spread_rows/pallas_call | solution.py:165
  116.6 5.0 slice_select_fusion.7
  121.5 12.4 %fusion.17 = f32[2,1536,768]{2,1,0:T(8,128)} fusion(bf16[1,1536,768]{2,1,0:T(8,128)(2,1)} %bitcast.272, bf16[1,1536,768]{2,1,0:T(8,128)(2,1)} %bitcast.271, bf16[1,2,768,768]{3,2,1,0:T(8,128)(2,1)S(1)} %copy-done, bf16[1,2,768,768]{3,2,1,0:T(8,128)(2,1)} %param.16), kind=kOutput, calls=%fused_computation.28 | convolution fusion | flops 7271350272 | bytes 18874368 | tf_op jit(solution)/shard_map/esh,ehd->esd/dot_general | solution.py:25
  136.0 4.1 convert.96
  143.7 39.5 %return_rows.4 = bf16[16,40,768]{2,1,0:T(8,128)(2,1)} custom-call(bf16[4,16,40,768]{3,2,1,0:T(8,128)(2,1)} %pad_maximum_fusion.3.part), custom_call_target="tpu_custom_call" | custom-call | tf_op jit(solution)/shard_map/return_rows/pallas_call | solution.py:251
  186.7 4.7 collective-permute-start
  191.5 5.2 collective-permute-done
  197.1 3.9 convolution_convert_fusion.1
  201.1 4.4 reshape.410
  210.5 2.4 convert_element_type.252
  217.9 35.0 %spread_rows.5 = bf16[4,16,40,768]{3,2,1,0:T(8,128)(2,1)} custom-call(bf16[16,40,768]{2,1,0:T(8,128)(2,1)} %bitcast.282), custom_call_target="tpu_custom_call" | custom-call | tf_op jit(solution)/shard_map/spread_rows/pallas_call | solution.py:165
  252.9 2.9 slice_select_fusion.5
  256.0 7.0 fusion.40
  262.9 8.3 %fusion.48 = f32[2,1536,768]{2,1,0:T(8,128)S(1)} fusion(bf16[1,2,768,768]{3,2,1,0:T(8,128)(2,1)S(1)} %copy-done, f32[2,1536,768]{2,1,0:T(8,128)} %fusion.40), kind=kOutput, calls=%fused_computation.66 | convolution fusion | flops 3645112320 | bytes 21233664 | tf_op jit(solution)/shard_map/esh,ehd->esd/dot_general | solution.py:25
  274.2 43.8 %return_rows.5 = bf16[16,40,768]{2,1,0:T(8,128)(2,1)} custom-call(bf16[4,16,40,768]{3,2,1,0:T(8,128)(2,1)} %pad_maximum_fusion.4.part), custom_call_target="tpu_custom_call" | custom-call | tf_op jit(solution)/shard_map/return_rows/pallas_call | solution.py:251
  319.7 2.8 fusion.162
  324.6 36.3 %spread_rows.6 = bf16[4,16,40,768]{3,2,1,0:T(8,128)(2,1)} custom-call(bf16[16,40,768]{2,1,0:T(8,128)(2,1)} %bitcast.257), custom_call_target="tpu_custom_call" | custom-call | tf_op jit(solution)/shard_map/spread_rows/pallas_call | solution.py:165
  360.9 5.0 slice_select_fusion.3
  365.8 15.9 %fusion.42 = f32[2,1536,768]{2,1,0:T(8,128)} fusion(f32[2,1536,768]{2,1,0:T(8,128)} %fusion.40, bf16[1,1536,768]{2,1,0:T(8,128)(2,1)} %bitcast.274, bf16[1,1536,768]{2,1,0:T(8,128)(2,1)} %bitcast.273, bf16[1,2,768,768]{3,2,1,0:T(8,128)(2,1)S(1)} %copy-done, bf16[1,2,768,768]{3,2,1,0:T(8,128)(2,1)} %param.16), kind=kOutput, calls=%fused_computation.54 | convolution fusion | flops 7297302528 | bytes 28311552 | tf_op jit(solution)/shard_map/esh,edh->esd/dot_general | solution.py:25
  383.8 4.1 convert.100
  390.3 38.7 %return_rows.6 = bf16[16,40,768]{2,1,0:T(8,128)(2,1)} custom-call(bf16[4,16,40,768]{3,2,1,0:T(8,128)(2,1)} %pad_maximum_fusion.5.part), custom_call_target="tpu_custom_call" | custom-call | tf_op jit(solution)/shard_map/return_rows/pallas_call | solution.py:251
  432.9 2.6 convolution_convert_fusion.15
  435.5 2.5 reshape.419
  438.1 3.1 fusion.170
  442.6 4.7 fusion.87
  447.3 4.9 fusion.90
  452.3 2.1 copy.157
  454.4 2.4 reshape.422
  456.8 2.1 copy.155
  458.9 2.4 reshape.421
  463.4 2.4 reshape.420
  465.8 3.8 multiply_reduce_fusion.10
  472.2 10.1 %collective-permute-done.1 = bf16[200,768]{1,0:T(8,128)(2,1)} collective-permute-done((bf16[200,768]{1,0:T(8,128)(2,1)}, bf16[200,768]{1,0:T(8,128)(2,1)}, u32[]{:S(2)}, u32[]{:S(2)}) %collective-permute-start.1) | collective-permute-done | bytes 307232 | tf_op jit(solution)/shard_map/ppermute | solution.py:41
  485.9 35.5 %spread_rows.7 = bf16[4,16,40,768]{3,2,1,0:T(8,128)(2,1)} custom-call(bf16[16,40,768]{2,1,0:T(8,128)(2,1)} %bitcast.258), custom_call_target="tpu_custom_call" | custom-call | tf_op jit(solution)/shard_map/spread_rows/pallas_call | solution.py:165
  521.4 2.8 slice_select_fusion.1
  524.2 11.9 %add_convert_fusion = bf16[2,1536,768]{2,1,0:T(8,128)(2,1)} fusion(f32[2,1536,768]{2,1,0:T(8,128)} %fusion.40, bf16[1,1536,768]{2,1,0:T(8,128)(2,1)S(1)} %bitcast.269, bf16[1,1536,768]{2,1,0:T(8,128)(2,1)S(1)} %bitcast.267, bf16[1,2,768,768]{3,2,1,0:T(8,128)(2,1)S(1)} %copy-done), kind=kOutput, calls=%fused_computation.18 | convolution fusion | flops 3673423872 | bytes 21233664 | tf_op jit(solution)/shard_map/esd,ehd->esh/dot_general | solution.py:25
  536.1 10.4 %fusion.58 = f32[1,2,768,768]{3,2,1,0:T(8,128)} fusion(bf16[1,1536,768]{2,1,0:T(8,128)(2,1)S(1)} %bitcast.270, bf16[1,1536,768]{2,1,0:T(8,128)(2,1)S(1)} %bitcast.268, f32[2,1536,768]{2,1,0:T(8,128)} %fusion.40), kind=kOutput, calls=%fused_computation.75 | convolution fusion | flops 3647471616 | bytes 18874368 | tf_op jit(solution)/shard_map/esh,esd->ehd/dot_general | solution.py:25
  546.5 8.3 %fusion.57 = f32[1,2,768,768]{3,2,1,0:T(8,128)} fusion(bf16[2,1536,768]{2,1,0:T(8,128)(2,1)} %add_convert_fusion, bf16[1,1536,768]{2,1,0:T(8,128)(2,1)S(1)} %bitcast.266, bf16[1,1536,768]{2,1,0:T(8,128)(2,1)S(1)} %bitcast.264), kind=kOutput, calls=%fused_computation.74 | convolution fusion | flops 3626237952 | bytes 14155776 | tf_op jit(solution)/shard_map/esd,esh->edh/dot_general | solution.py:25
  554.9 4.0 fusion.51
  562.5 43.7 %return_rows.7 = bf16[16,40,768]{2,1,0:T(8,128)(2,1)} custom-call(bf16[4,16,40,768]{3,2,1,0:T(8,128)(2,1)} %pad_maximum_fusion.6.part), custom_call_target="tpu_custom_call" | custom-call | tf_op jit(solution)/shard_map/return_rows/pallas_call | solution.py:251
  610.8 2.5 convolution_convert_fusion.14
  613.3 2.4 reshape.427
  615.7 3.2 fusion.167
  620.3 4.7 fusion.93
  624.9 4.8 fusion.96
  629.7 2.8 convolution_convert_fusion.3
  633.5 2.4 reshape.429
  635.9 2.1 copy.160
  638.0 2.4 reshape.428
  640.4 2.1 copy.163
  642.5 2.6 reshape.430
  648.0 4.2 fusion.148
  658.2 5.2 concatenate.85
  666.0 2.8 pad_maximum_fusion.part
  668.7 38.6 %reduce_dense.1 = f32[2,2,24,1664]{3,2,1,0:T(8,128)} custom-call(bf16[2,16,2,24,1664]{4,3,2,1,0:T(8,128)(2,1)} %pad_maximum_fusion.part), custom_call_target="tpu_custom_call" | custom-call | tf_op jit(solution)/shard_map/reduce_dense/pallas_call | solution.py:570
  710.5 2.2 fusion.199
  (234 shorter events, 107.1 us)
Async XLA Ops:
  0.6 120.9 %copy-start = (bf16[1,2,768,768]{3,2,1,0:T(8,128)(2,1)S(1)}, bf16[1,2,768,768]{3,2,1,0:T(8,128)(2,1)}, u32[]{:S(2)}) copy-start(bf16[1,2,768,768]{3,2,1,0:T(8,128)(2,1)} %param.17) | copy-start | bytes 7077892
  47.2 1.7 copy-start.8
  51.9 144.8 %copy-start.4 = (bf16[200,768]{1,0:T(8,128)(2,1)}, bf16[200,768]{1,0:T(8,128)(2,1)S(1)}, u32[]{:S(2)}) copy-start(bf16[200,768]{1,0:T(8,128)(2,1)S(1)} %reshape_squeeze.3) | copy-start | bytes 921604
  54.4 2.6 copy-start.32
  55.9 1.0 copy-start.33
  55.9 141.2 %copy-start.35 = (f32[768]{0:T(1024)}, f32[768]{0:T(1024)S(1)}, u32[]{:S(2)}) copy-start(f32[768]{0:T(1024)S(1)} %get-tuple-element.63) | copy-start | bytes 9220
  81.7 0.8 copy-start.17
  186.7 10.0 %collective-permute-start = (bf16[200,768]{1,0:T(8,128)(2,1)S(1)}, bf16[200,768]{1,0:T(8,128)(2,1)S(1)}, u32[]{:S(2)}, u32[]{:S(2)}) collective-permute-start(bf16[200,768]{1,0:T(8,128)(2,1)S(1)} %fusion.102), channel_id=1, source_target_pairs={{0,64},{1,65},{2,66},{3,67},{4,68},{5,69},{6,70},{7,71},{8,72},{9,... | collective-permute-start | bytes 921608 | tf_op jit(solution)/shard_map/ppermute | solution.py:41
  207.6 1.5 copy-start.13
  207.6 1.5 copy-start.22
  207.6 1.5 copy-start.23
  208.2 1.2 copy-start.1
  215.2 1.3 copy-start.24
  252.9 3.1 copy-start.37
  255.8 7.2 copy-start.28
  255.8 7.1 copy-start.30
  318.0 4.6 copy-start.5
  319.7 3.4 copy-start.9
  428.9 4.0 copy-start.6
  432.1 0.8 copy-start.26
  438.1 3.2 copy-start.2
  438.1 3.2 copy-start.15
  465.8 4.1 copy-start.7
  465.8 4.1 copy-start.27
  470.9 11.4 %collective-permute-start.1 = (bf16[200,768]{1,0:T(8,128)(2,1)}, bf16[200,768]{1,0:T(8,128)(2,1)}, u32[]{:S(2)}, u32[]{:S(2)}) collective-permute-start(bf16[200,768]{1,0:T(8,128)(2,1)} %fusion.145), channel_id=1, source_target_pairs={{64,0},{65,1},{66,2},{67,3},{68,4},{69,5},{70,6},{71,7},{72,8},{73... | collective-permute-start | bytes 921608 | tf_op jit(solution)/shard_map/ppermute | solution.py:41
  483.9 2.0 copy-start.18
  536.1 10.4 %copy-start.29 = (bf16[64,24,768]{2,1,0:T(8,128)(2,1)S(1)}, bf16[64,24,768]{2,1,0:T(8,128)(2,1)}, u32[]{:S(2)}) copy-start(bf16[64,24,768]{2,1,0:T(8,128)(2,1)} %copy-done.28) | copy-start | bytes 7077892
  536.1 10.4 %copy-start.31 = (bf16[64,24,768]{2,1,0:T(8,128)(2,1)S(1)}, bf16[64,24,768]{2,1,0:T(8,128)(2,1)}, u32[]{:S(2)}) copy-start(bf16[64,24,768]{2,1,0:T(8,128)(2,1)} %copy-done.30) | copy-start | bytes 7077892
  546.5 8.4 %copy-start.38 = (bf16[1,2,768,768]{3,2,1,0:T(8,128)(2,1)S(1)}, bf16[1,2,768,768]{3,2,1,0:T(8,128)(2,1)}, u32[]{:S(2)}) copy-start(bf16[1,2,768,768]{3,2,1,0:T(8,128)(2,1)} %param.16) | copy-start | bytes 7077892
  546.5 8.4 %copy-start.39 = (bf16[2,1536,768]{2,1,0:T(8,128)(2,1)S(1)}, bf16[2,1536,768]{2,1,0:T(8,128)(2,1)}, u32[]{:S(2)}) copy-start(bf16[2,1536,768]{2,1,0:T(8,128)(2,1)} %add_convert_fusion) | copy-start | bytes 14155780
  559.1 1.0 copy-start.25
  606.3 3.5 copy-start.19
  610.0 0.8 copy-start.11
  615.7 3.2 copy-start.3
  615.7 3.2 copy-start.14
  629.7 2.8 copy-start.34
  648.0 4.2 copy-start.36
  663.4 2.1 copy-start.20
  663.4 2.4 copy-start.21
  707.4 3.1 copy-start.10
  707.4 3.1 copy-start.12
  707.4 3.1 copy-start.16
